TPU v7x, 512 devices: a whole 4x8x8 slice. The times are simulated.
512 devices in a mesh: dp: 32 (over z_hi, y, core), seq: 16 (over z_lo, x).
Axes of the slice: x: 4, y: 8, z: 8 (z_hi: 2, z_lo: 4; z = z_hi * 4 + z_lo), core: 2. Of those that a mesh axis runs over, the one named last changes fastest.
Arguments:
- img_qkv: bfloat16 [32, 1792, 3, 2048], P('dp', 'seq'), may hold values from -6 to 6
- txt_qkv: bfloat16 [32, 256, 3, 2048], P('dp', 'seq'), may hold values from -6 to 6
- img_cot: bfloat16 [32, 1792, 2048], P('dp', 'seq'), may hold values from -48 to 48
- txt_cot: bfloat16 [32, 256, 2048], P('dp', 'seq'), may hold values from -48 to 48
- norm_gains: float32 [4, 128], replicated, may hold values from 0.5 to 2
Outputs:
- img_out: bfloat16 [32, 1792, 2048], P('dp', 'seq')
- txt_out: bfloat16 [32, 256, 2048], P('dp', 'seq')
- img_grad: bfloat16 [32, 1792, 3, 2048], P('dp', 'seq')
- txt_grad: bfloat16 [32, 256, 3, 2048], P('dp', 'seq')
- gain_grad: float32 [512], P('dp')
All inputs are finite; a program needn't handle non-finite values.
Results may differ from a plain program's by a relative error of at most 0.012.
The roundings to bfloat16 on the way count: a program that leaves them out, or rounds other values in their place, can miss the bound.
Values may be sent and summed in bfloat16 or wider, within the bound.
A program may use at most 128 MiB of HBM per device.

v0:
```python
import math

import jax
import jax.numpy as jnp
from jax import lax
from jax.sharding import PartitionSpec as P

HD = 128
GRID_W = 64


EPSILON = 1e-06


def rope_tables(seq_len, text_len, grid_w, head_dim):
    position = jnp.arange(seq_len, dtype=jnp.int32)
    image_pos = jnp.maximum(position - text_len, 0)
    image_col = (position >= text_len).astype(jnp.float32)
    row_pos = (image_pos // grid_w).astype(jnp.float32) * image_col
    col_pos = (image_pos % grid_w).astype(jnp.float32) * image_col
    time_dims = head_dim // 8
    axis_dims = (head_dim - time_dims) // 2
    channel = jnp.arange(head_dim, dtype=jnp.int32)
    in_rows = (channel >= time_dims) & (channel < time_dims + axis_dims)
    in_cols = channel >= time_dims + axis_dims
    within = jnp.where(in_cols, channel - time_dims - axis_dims, channel - time_dims)
    within = jnp.maximum(within, 0) // 2
    frequency = jnp.power(jnp.float32(10000.0), -2.0 * within.astype(jnp.float32) / axis_dims)
    angles = jnp.where(in_rows[None, :], row_pos[:, None] * frequency[None, :], jnp.float32(0.0))
    angles = jnp.where(in_cols[None, :], col_pos[:, None] * frequency[None, :], angles)
    even_lane = (channel % 2 == 0)[None, :]
    return (jnp.cos(angles), jnp.sin(angles), even_lane, image_col[:, None])


def rms_rows(values_in):
    inverse = lax.rsqrt(jnp.mean(values_in * values_in, axis=-1, keepdims=True) + EPSILON)
    return (values_in * inverse, inverse)


def rms_back(grad_hat, hat_vals, inverse):
    middle = jnp.mean(grad_hat * hat_vals, axis=-1, keepdims=True)
    return (grad_hat - hat_vals * middle) * inverse


def rotate(values_in, tables):
    cos_t, sin_t, even_lane, image_col = tables
    following = jnp.roll(values_in, -1, axis=-1)
    preceding = jnp.roll(values_in, 1, axis=-1)
    turned = jnp.where(even_lane, -following, preceding)
    return values_in * cos_t + turned * sin_t


def unrotate(grad_in, tables):
    cos_t, sin_t, even_lane, image_col = tables
    scaled = grad_in * sin_t
    following = jnp.roll(scaled, -1, axis=-1)
    preceding = jnp.roll(scaled, 1, axis=-1)
    turned = jnp.where(even_lane, following, -preceding)
    return grad_in * cos_t + turned


def head_pass(q_raw, k_raw, value, d_out, norm_gains, tables, n_blocks):
    image_col = tables[3]
    seq_len, head_dim = q_raw.shape
    attn_scale = 1.0 / math.sqrt(head_dim)
    q_hat, q_inv = rms_rows(q_raw)
    k_hat, k_inv = rms_rows(k_raw)
    q_gain = jnp.where(image_col > 0.5, norm_gains[0][None, :], norm_gains[2][None, :])
    k_gain = jnp.where(image_col > 0.5, norm_gains[1][None, :], norm_gains[3][None, :])
    q_rot = rotate(q_hat * q_gain, tables).astype(jnp.bfloat16)
    k_rot = rotate(k_hat * k_gain, tables).astype(jnp.bfloat16)
    block_rows = seq_len // n_blocks
    contract_last = (((1,), (1,)), ((), ()))
    contract_first = (((0,), (0,)), ((), ()))

    def block_step(pieces):
        q_block, d_block = pieces
        scores = (
            lax.dot_general(q_block, k_rot, contract_last, preferred_element_type=jnp.float32)
            * attn_scale
        )
        exp_scores = jnp.exp(scores)
        row_sum = jnp.sum(exp_scores, axis=1, keepdims=True)
        prob_half = (exp_scores / row_sum).astype(jnp.bfloat16)
        out_block = jnp.dot(prob_half, value, preferred_element_type=jnp.float32).astype(
            jnp.bfloat16
        )
        row_delta = jnp.sum(
            d_block.astype(jnp.float32) * out_block.astype(jnp.float32), axis=1, keepdims=True
        )
        d_prob = lax.dot_general(d_block, value, contract_last, preferred_element_type=jnp.float32)
        d_score = (exp_scores / row_sum * (d_prob - row_delta) * attn_scale).astype(jnp.bfloat16)
        return (out_block, prob_half, d_score)

    q_blocks = q_rot.reshape(n_blocks, block_rows, head_dim)
    d_blocks = d_out.reshape(n_blocks, block_rows, head_dim)
    out_blocks, prob_blocks, score_blocks = lax.map(block_step, (q_blocks, d_blocks))
    attn_out = out_blocks.reshape(seq_len, head_dim)
    prob_all = prob_blocks.reshape(seq_len, seq_len)
    d_score_all = score_blocks.reshape(seq_len, seq_len)
    d_value = lax.dot_general(prob_all, d_out, contract_first, preferred_element_type=jnp.float32)
    dq_rot = jnp.dot(d_score_all, k_rot, preferred_element_type=jnp.float32)
    dk_rot = lax.dot_general(d_score_all, q_rot, contract_first, preferred_element_type=jnp.float32)
    dq_norm = unrotate(dq_rot, tables)
    dk_norm = unrotate(dk_rot, tables)
    text_col = 1.0 - image_col
    gain_terms = jnp.stack(
        [
            jnp.sum(dq_norm * q_hat * image_col, axis=0),
            jnp.sum(dk_norm * k_hat * image_col, axis=0),
            jnp.sum(dq_norm * q_hat * text_col, axis=0),
            jnp.sum(dk_norm * k_hat * text_col, axis=0),
        ]
    )
    d_query = rms_back(dq_norm * q_gain, q_hat, q_inv).astype(jnp.bfloat16)
    d_key = rms_back(dk_norm * k_gain, k_hat, k_inv).astype(jnp.bfloat16)
    packed = jnp.stack([d_query, d_key, d_value.astype(jnp.bfloat16), attn_out], axis=1)
    return (packed, gain_terms)


def per_device(img_qkv, txt_qkv, img_cot, txt_cot, norm_gains):
    seq_devices = lax.axis_size("seq")
    data_devices = lax.axis_size("dp")
    img_proj, txt_proj = (
        lax.all_to_all(img_qkv, "seq", split_axis=3, concat_axis=1, tiled=True),
        lax.all_to_all(txt_qkv, "seq", split_axis=3, concat_axis=1, tiled=True),
    )
    img_grad_in, txt_grad_in = (
        lax.all_to_all(img_cot, "seq", split_axis=2, concat_axis=1, tiled=True),
        lax.all_to_all(txt_cot, "seq", split_axis=2, concat_axis=1, tiled=True),
    )
    text_len = txt_proj.shape[1]
    joint = jnp.concatenate([txt_proj[0], img_proj[0]], axis=0)
    joint_cot = jnp.concatenate([txt_grad_in[0], img_grad_in[0]], axis=0)
    seq_len = joint.shape[0]
    head_dim = HD
    local_heads = joint.shape[2] // head_dim
    tables = rope_tables(seq_len, text_len, GRID_W, head_dim)
    n_blocks = max(1, seq_len // 512)
    packed, gain_terms = head_pass(
        joint[:, 0, 0:head_dim].astype(jnp.float32),
        joint[:, 1, 0:head_dim].astype(jnp.float32),
        joint[:, 2, 0:head_dim],
        joint_cot,
        norm_gains,
        tables,
        n_blocks,
    )
    txt_back = packed[None, :text_len]
    img_back = packed[None, text_len:]
    img_tokens, txt_tokens = (
        lax.all_to_all(img_back, "seq", split_axis=1, concat_axis=3, tiled=True),
        lax.all_to_all(txt_back, "seq", split_axis=1, concat_axis=3, tiled=True),
    )
    img_out = img_tokens[:, :, 3, :]
    txt_out = txt_tokens[:, :, 3, :]
    img_grad = img_tokens[:, :, 0:3, :]
    txt_grad = txt_tokens[:, :, 0:3, :]
    grad_scale = 1.0 / math.sqrt(data_devices * seq_len * local_heads * seq_devices)
    partial_grad = (gain_terms * grad_scale).reshape(4 * head_dim)
    summed = lax.psum(partial_grad, "seq")
    gain_grad = lax.psum_scatter(summed, "dp", scatter_dimension=0, tiled=True)
    return (img_out, txt_out, img_grad, txt_grad, gain_grad)


def solution(mesh):
    in_specs = (
        P("dp", "seq", None, None),
        P("dp", "seq", None, None),
        P("dp", "seq", None),
        P("dp", "seq", None),
        P(),
    )
    out_specs = (
        P("dp", "seq", None),
        P("dp", "seq", None),
        P("dp", "seq", None, None),
        P("dp", "seq", None, None),
        P("dp"),
    )
    return jax.shard_map(
        per_device, mesh=mesh, in_specs=in_specs, out_specs=out_specs, check_vma=False
    )
```

profile of v0, /device:TPU:2, one launch (start us, length us, event | category | flops | bytes accessed | tf_op | source)
XLA Modules:
  0.0 399.0 jit_solution(10600250610665582752)
XLA Ops:
  0.6 2.0 copy.70
  3.1 11.5 %reduce.9 = bf16[2048,16]{1,0:T(8,128)(2,1)S(1)} reduce(bf16[2048,1,16]{2,1,0:T(2,128)(2,1)S(1)} %bitcast.205, bf16[]{:T(256)} %broadcast.812), dimensions={1}, to_apply=%bitcast.165.reduce_sub_computation | reduce | bytes 131074
  14.7 1.2 reshape.852
  15.9 10.3 %all-to-all-start.2 = ((bf16[16,2,1024]{2,1,0:T(2,128)(2,1)}), bf16[16,2,1024]{2,1,0:T(2,128)(2,1)S(1)}, u32[]{:S(2)}, u32[]{:S(2)}) async-start(bf16[16,2,1024]{2,1,0:T(2,128)(2,1)} %reshape.852), calls=%async_computation.2 | async-start | bytes 131072 | tf_op jit(solution)/shard_map/all_to_all | solution.py:130
  26.1 2.6 copy.57
  28.7 2.7 reshape.848
  31.4 1.7 all-to-all-done.2
  33.2 6.3 %all-to-all-start = ((bf16[16,2,3072]{2,1,0:T(2,128)(2,1)}), bf16[16,2,3072]{2,1,0:T(2,128)(2,1)S(1)}, u32[]{:S(2)}, u32[]{:S(2)}) async-start(bf16[16,2,3072]{2,1,0:T(2,128)(2,1)} %reshape.848), calls=%async_computation | async-start | bytes 393216 | tf_op jit(solution)/shard_map/all_to_all | solution.py:126
  39.5 2.3 copy.73
  41.9 11.5 %reduce.8 = bf16[2048,112]{1,0:T(8,128)(2,1)S(1)} reduce(bf16[2048,1,112]{2,1,0:T(2,128)(2,1)S(1)} %bitcast.206, bf16[]{:T(256)} %broadcast.812), dimensions={1}, to_apply=%bitcast.163.reduce_sub_computation | reduce | bytes 917506
  53.4 1.8 reshape.850
  55.3 7.7 %all-to-all-start.3 = ((bf16[16,2,7168]{2,1,0:T(2,128)(2,1)}), bf16[16,2,7168]{2,1,0:T(2,128)(2,1)S(1)}, u32[]{:S(2)}, u32[]{:S(2)}) async-start(bf16[16,2,7168]{2,1,0:T(2,128)(2,1)} %reshape.850), calls=%async_computation.3 | async-start | bytes 917504 | tf_op jit(solution)/shard_map/all_to_all | solution.py:129
  62.9 2.6 copy.60
  65.5 9.2 %all-to-all-done.3 = bf16[16,2,7168]{2,1,0:T(2,128)(2,1)S(1)} async-done(((bf16[16,2,7168]{2,1,0:T(2,128)(2,1)}), bf16[16,2,7168]{2,1,0:T(2,128)(2,1)S(1)}, u32[]{:S(2)}, u32[]{:S(2)}) %all-to-all-start.3) | async-done | bytes 458784 | tf_op jit(solution)/shard_map/all_to_all | solution.py:129
  75.4 6.0 %all-to-all-start.1 = ((bf16[1,112,3,2048]{1,2,0,3:T(4,128)(2,1)}), bf16[1,112,3,2048]{1,2,0,3:T(4,128)(2,1)S(1)}, u32[]{:S(2)}, u32[]{:S(2)}) async-start(bf16[1,112,3,2048]{1,2,0,3:T(4,128)(2,1)} %copy.60), calls=%async_computation.1 | async-start | bytes 4194304 | tf_op jit(solution)/shard_map/all_to_all | solution.py:125
  84.0 0.9 reshape.853
  85.5 4.2 %reshape.849 = bf16[2048,1,3,16]{3,2,1,0:T(4,128)(2,1)} reshape(bf16[16,2,3072]{2,1,0:T(2,128)(2,1)} %copy-done.15) | data formatting | bytes 393216
  89.7 2.8 copy.89
  92.6 2.8 reshape.851
  95.4 0.9 copy.97
  96.3 1.4 copy.95
  98.6 0.9 pad_maximum_fusion.2
  99.5 21.8 %all-to-all-done.1 = bf16[1,112,3,2048]{1,2,0,3:T(4,128)(2,1)S(1)} async-done(((bf16[1,112,3,2048]{1,2,0,3:T(4,128)(2,1)}), bf16[1,112,3,2048]{1,2,0,3:T(4,128)(2,1)S(1)}, u32[]{:S(2)}, u32[]{:S(2)}) %all-to-all-start.1) | async-done | bytes 1376288 | tf_op jit(solution)/shard_map/all_to_all | solution.py:125
  121.3 2.3 copy.91
  123.6 1.8 copy.64
  125.9 1.6 slice_bitcast_fusion.11
  128.2 5.9 %fusion.33 = (bf16[2048,128]{0,1:T(8,128)(2,1)}, f32[2048,128]{0,1:T(8,128)S(1)}) fusion(f32[2048,1]{0,1:T(1,128)S(1)} %get-tuple-element.142, f32[2048,127]{0,1:T(8,128)S(1)} %get-tuple-element.145, f32[2048,127]{0,1:T(8,128)S(1)} %get-tuple-element.144, f32[2048,1]{0,1:T(1,128)S(1)} %get-tuple-element.141, f32[2048]{0:T(1024)S(1)} %get-tuple-element.161, ...), kind=kLoop, calls=%fused_computation.55 | loop fusion | flops 5242880 | bytes 4756352 | tf_op jit(solution)/shard_map/convert_element_type | solution.py:71
  134.2 2.2 slice_bitcast_fusion.13
  137.2 1.7 fusion.54
  139.0 2.6 copy.93
  141.6 2.6 copy.94
  144.2 1.8 concatenate.120
  146.0 1.8 concatenate.121
  148.1 2.1 copy.77
  150.3 7.8 %fusion.29 = bf16[4,512,128]{2,1,0:T(8,128)(2,1)S(1)} fusion(f32[4,512,1]{2,1,0:T(8,128)} %concatenate.120, f32[4,512,127]{2,1,0:T(8,128)} %bitcast.210, f32[4,512,127]{2,1,0:T(8,128)} %bitcast.211, f32[4,512,1]{2,1,0:T(8,128)} %concatenate.121, f32[4,512,128]{2,1,0:T(8,128)S(1)} %bitcast.209, f32[4,512]{1,0:T(4,128)S(1)} %copy-done.28, ...), kind=kLoop, calls=%fused_computation.50 | loop fusion | flops 3932160 | bytes 3698560 | tf_op jit(solution)/shard_map/convert_element_type | solution.py:70
  158.1 41.7 %while.14 = (s32[]{:T(128)}, bf16[4,512,128]{1,2,0:T(8,128)(2,1)}, bf16[4,512,2048]{2,1,0:T(8,128)(2,1)}, bf16[4,512,2048]{2,1,0:T(8,128)(2,1)}, bf16[4,512,128]...) while((s32[]{:T(128)}, bf16[4,512,128]{1,2,0:T(8,128)(2,1)}, ...), condition=%wide.region_5.6_spmd, body=%wide.region_2.5_spmd.sunk | while | flops 820313088 | bytes 65812748 | solution.py:97
  159.4 1.7 bitcast_dynamic-update-slice_fusion.4
  161.2 5.0 %fusion.134 = bf16[4,512,2048]{2,1,0:T(8,128)(2,1)} fusion(bf16[4,512,2048]{2,1,0:T(8,128)(2,1)} %get-tuple-element.237, s32[]{:T(128)} %get-tuple-element.234, bf16[2048,128]{1,0:T(8,128)(2,1)} %get-tuple-element.249, f32[512]{0:T(512)S(1)} %multiply_reduce_fusion.7, bf16[4,512,128]{2,1,0:T(8,128)(2,1)S(1)} %copy-done.2, ...), kind=kOutput, calls=%fused_computation.5.clone.1 | convolution fusion | flops 274726912 | bytes 6951936 | tf_op jit(solution)/shard_map/while/body/eval_jaxpr/dot_general | solution.py:91
  166.3 2.1 bitcast_dynamic-update-slice_fusion.5
  169.6 1.7 bitcast_dynamic-update-slice_fusion.4
  171.5 5.1 %fusion.134 = bf16[4,512,2048]{2,1,0:T(8,128)(2,1)} fusion(bf16[4,512,2048]{2,1,0:T(8,128)(2,1)} %get-tuple-element.237, s32[]{:T(128)} %get-tuple-element.234, bf16[2048,128]{1,0:T(8,128)(2,1)} %get-tuple-element.249, f32[512]{0:T(512)S(1)} %multiply_reduce_fusion.7, bf16[4,512,128]{2,1,0:T(8,128)(2,1)S(1)} %copy-done.2, ...), kind=kOutput, calls=%fused_computation.5.clone.1 | convolution fusion | flops 274726912 | bytes 6951936 | tf_op jit(solution)/shard_map/while/body/eval_jaxpr/dot_general | solution.py:91
  176.6 2.1 bitcast_dynamic-update-slice_fusion.5
  178.8 0.8 fusion.133
  180.0 1.7 bitcast_dynamic-update-slice_fusion.4
  181.9 5.0 %fusion.134 = bf16[4,512,2048]{2,1,0:T(8,128)(2,1)} fusion(bf16[4,512,2048]{2,1,0:T(8,128)(2,1)} %get-tuple-element.237, s32[]{:T(128)} %get-tuple-element.234, bf16[2048,128]{1,0:T(8,128)(2,1)} %get-tuple-element.249, f32[512]{0:T(512)S(1)} %multiply_reduce_fusion.7, bf16[4,512,128]{2,1,0:T(8,128)(2,1)S(1)} %copy-done.2, ...), kind=kOutput, calls=%fused_computation.5.clone.1 | convolution fusion | flops 274726912 | bytes 6951936 | tf_op jit(solution)/shard_map/while/body/eval_jaxpr/dot_general | solution.py:91
  186.9 2.2 bitcast_dynamic-update-slice_fusion.5
  190.3 1.7 bitcast_dynamic-update-slice_fusion.4
  192.1 5.0 %fusion.134 = bf16[4,512,2048]{2,1,0:T(8,128)(2,1)} fusion(bf16[4,512,2048]{2,1,0:T(8,128)(2,1)} %get-tuple-element.237, s32[]{:T(128)} %get-tuple-element.234, bf16[2048,128]{1,0:T(8,128)(2,1)} %get-tuple-element.249, f32[512]{0:T(512)S(1)} %multiply_reduce_fusion.7, bf16[4,512,128]{2,1,0:T(8,128)(2,1)S(1)} %copy-done.2, ...), kind=kOutput, calls=%fused_computation.5.clone.1 | convolution fusion | flops 274726912 | bytes 6951936 | tf_op jit(solution)/shard_map/while/body/eval_jaxpr/dot_general | solution.py:91
  197.1 2.2 bitcast_dynamic-update-slice_fusion.5
  199.9 10.5 %fusion.57 = f32[2048,128]{0,1:T(8,128)S(1)} fusion(bf16[2048,2048]{1,0:T(8,128)(2,1)} %bitcast.232, bf16[2048,1,128]{0,2,1:T(8,128)(2,1)S(1)} %get-tuple-element.114, f32[2048,1,1]{0,2,1:T(1,128)} %get-tuple-element.140, f32[2048,1,127]{0,2,1:T(8,128)} %get-tuple-element.146, f32[2048,1,127]{0,2,1:T(8,128)S(1)} %copy-done.12, ...), kind=kOutput, calls=%fused_computation.97 | convolution fusion | flops 1077936128 | bytes 12087168 | tf_op jit(solution)/shard_map/dot_general | solution.py:102
  210.5 9.0 %fusion.47 = (f32[2048,128]{0,1:T(8,128)S(1)}, f32[2048,128]{0,1:T(8,128)S(1)}, f32[2048,128]{0,1:T(8,128)S(1)}) fusion(f32[2048]{0:T(1024)S(1)} %copy-done.26, f32[128]{0:T(128)S(1)} %copy-done.50, f32[2048]{0:T(1024)S(1)} %copy-done.24, pred[128]{0:T(512)(128)(4,1)S(1)} %copy-done.53, pred[128]{0:T(512)(128)(4,1)S(1)} %copy-done.47, ...), kind=kOutput, calls=%fused_computation.85 | convolution fusion | flops 1079508992 | bytes 15232896 | tf_op jit(solution)/shard_map/dot_general | solution.py:103
  220.2 9.2 %multiply_reduce_fusion.3 = (f32[128]{0:T(128)S(1)}, f32[128]{0:T(128)S(1)}, f32[2048]{0:T(1024)S(1)}, f32[2048]{0:T(1024)S(1)}, f32[128]{0:T(128)S(1)}, /*index...) fusion(bf16[2048,1,128]{0,2,1:T(8,128)(2,1)S(1)} %get-tuple-element.114, f32[2048]{0:T(1024)S(1)} %copy-done.29, ...), kind=kLoop, calls=%fused_computation.75 | loop fusion | flops 9956864 | bytes 9509760 | tf_op jit(solution)/shard_map/reduce_sum | solution.py:110
  229.5 2.1 fusion.11
  232.5 2.0 fusion.50
  234.8 0.9 copy.84
  235.7 12.1 %all-to-all-start.5 = ((bf16[1,256,4,128]{3,2,0,1:T(4,128)(2,1)}), bf16[1,256,4,128]{3,2,0,1:T(4,128)(2,1)S(1)}, u32[]{:S(2)}, u32[]{:S(2)}) async-start(bf16[1,256,4,128]{3,2,0,1:T(4,128)(2,1)} %copy.84), calls=%async_computation.5 | async-start | bytes 524288 | tf_op jit(solution)/shard_map/all_to_all | solution.py:153
  247.8 1.4 slice_bitcast_fusion
  249.3 4.1 %copy.81 = bf16[1,1792,4,128]{3,2,0,1:T(4,128)(2,1)} copy(bf16[1,1792,4,128]{1,3,2,0:T(8,128)(2,1)} %slice_bitcast_fusion) | data formatting | bytes 3670016 | tf_op jit(solution)/shard_map/broadcast_in_dim | solution.py:150
  253.3 3.1 all-to-all-done.5
  256.4 5.0 %all-to-all-start.4 = ((bf16[1,1792,4,128]{3,2,0,1:T(4,128)(2,1)}), bf16[1,1792,4,128]{3,2,0,1:T(4,128)(2,1)S(1)}, u32[]{:S(2)}, u32[]{:S(2)}) async-start(bf16[1,1792,4,128]{3,2,0,1:T(4,128)(2,1)} %copy.81), calls=%async_computation.4 | async-start | bytes 3670016 | tf_op jit(solution)/shard_map/all_to_all | solution.py:152
  261.4 1.3 dynamic-slice
  263.3 92.2 %all-reduce = f32[512]{0:T(512)S(1)} all-reduce(f32[512]{0:T(512)S(1)} %fusion.101), channel_id=2, replica_groups=mesh['dp'=32,'seq'=16] {'dp'}, use_global_device_ids=true, to_apply=%region_13.14.clone | all-reduce | flops 512 | bytes 4096
  355.6 39.0 %psum.8 = f32[16]{0:T(128)} all-reduce(f32[16]{0:T(128)S(1)} %dynamic-slice.1), channel_id=1, replica_groups=mesh['dp'=32,'seq'=16] {'seq'}, use_global_device_ids=true, to_apply=%region_12.13 | all-reduce | flops 16 | bytes 128 | tf_op jit(solution)/shard_map/psum | solution.py:161
  396.8 1.2 slice.143
  (222 shorter events, 17.3 us)
Async XLA Ops:
  15.9 17.3 %all-to-all-start.2 = ((bf16[16,2,1024]{2,1,0:T(2,128)(2,1)}), bf16[16,2,1024]{2,1,0:T(2,128)(2,1)S(1)}, u32[]{:S(2)}, u32[]{:S(2)}) async-start(bf16[16,2,1024]{2,1,0:T(2,128)(2,1)} %reshape.852), calls=%async_computation.2 | async-start | bytes 131072 | tf_op jit(solution)/shard_map/all_to_all | solution.py:130
  28.7 34.2 %copy-start.11 = (bf16[1,112,3,2048]{3,1,2,0:T(8,128)(2,1)S(1)}, bf16[1,112,3,2048]{3,1,2,0:T(8,128)(2,1)}, u32[]{:S(2)}) copy-start(bf16[1,112,3,2048]{3,1,2,0:T(8,128)(2,1)} %param.7) | copy-start | bytes 4128772
  33.2 22.1 %all-to-all-start = ((bf16[16,2,3072]{2,1,0:T(2,128)(2,1)}), bf16[16,2,3072]{2,1,0:T(2,128)(2,1)S(1)}, u32[]{:S(2)}, u32[]{:S(2)}) async-start(bf16[16,2,3072]{2,1,0:T(2,128)(2,1)} %reshape.848), calls=%async_computation | async-start | bytes 393216 | tf_op jit(solution)/shard_map/all_to_all | solution.py:126
  55.2 28.7 %copy-start.57 = (f32[4,128]{1,0:T(4,128)S(1)}, f32[4,128]{1,0:T(4,128)}, u32[]{:S(2)}) copy-start(f32[4,128]{1,0:T(4,128)} %param.11) | copy-start | bytes 6148
  55.2 19.4 %copy-start.15 = (bf16[16,2,3072]{2,1,0:T(2,128)(2,1)}, bf16[16,2,3072]{2,1,0:T(2,128)(2,1)S(1)}, u32[]{:S(2)}) copy-start(bf16[16,2,3072]{2,1,0:T(2,128)(2,1)S(1)} %all-to-all-done) | copy-start | bytes 589828
  55.3 19.4 %all-to-all-start.3 = ((bf16[16,2,7168]{2,1,0:T(2,128)(2,1)}), bf16[16,2,7168]{2,1,0:T(2,128)(2,1)S(1)}, u32[]{:S(2)}, u32[]{:S(2)}) async-start(bf16[16,2,7168]{2,1,0:T(2,128)(2,1)} %reshape.850), calls=%async_computation.3 | async-start | bytes 917504 | tf_op jit(solution)/shard_map/all_to_all | solution.py:129
  75.4 45.9 %all-to-all-start.1 = ((bf16[1,112,3,2048]{1,2,0,3:T(4,128)(2,1)}), bf16[1,112,3,2048]{1,2,0,3:T(4,128)(2,1)S(1)}, u32[]{:S(2)}, u32[]{:S(2)}) async-start(bf16[1,112,3,2048]{1,2,0,3:T(4,128)(2,1)} %copy.60), calls=%async_computation.1 | async-start | bytes 4194304 | tf_op jit(solution)/shard_map/all_to_all | solution.py:125
  81.4 46.7 %copy-start.45 = (pred[128]{0:T(512)(128)(4,1)}, pred[128]{0:T(512)(128)(4,1)S(1)}, u32[]{:S(2)}) copy-start(pred[128]{0:T(512)(128)(4,1)S(1)} %iota_compare_fusion.1) | copy-start | bytes 388
  81.5 46.7 %copy-start.48 = (f32[128]{0:T(128)}, f32[128]{0:T(128)S(1)}, u32[]{:S(2)}) copy-start(f32[128]{0:T(128)S(1)} %multiply_power_fusion) | copy-start | bytes 1540
  81.5 46.6 %copy-start.51 = (pred[128]{0:T(512)(128)(4,1)}, pred[128]{0:T(512)(128)(4,1)S(1)}, u32[]{:S(2)}) copy-start(pred[128]{0:T(512)(128)(4,1)S(1)} %get-tuple-element.162) | copy-start | bytes 388
  81.5 46.6 %copy-start.54 = (pred[128]{0:T(512)(128)(4,1)}, pred[128]{0:T(512)(128)(4,1)S(1)}, u32[]{:S(2)}) copy-start(pred[128]{0:T(512)(128)(4,1)S(1)} %get-tuple-element.163) | copy-start | bytes 388
  83.3 44.9 %copy-start.23 = (f32[2048]{0:T(1024)}, f32[2048]{0:T(1024)S(1)}, u32[]{:S(2)}) copy-start(f32[2048]{0:T(1024)S(1)} %get-tuple-element.160) | copy-start | bytes 24580
  83.3 44.9 %copy-start.25 = (f32[2048]{0:T(1024)}, f32[2048]{0:T(1024)S(1)}, u32[]{:S(2)}) copy-start(f32[2048]{0:T(1024)S(1)} %get-tuple-element.161) | copy-start | bytes 24580
  83.9 44.2 %copy-start.31 = (f32[128]{0:T(128)}, f32[128]{0:T(128)S(1)}, u32[]{:S(2)}) copy-start(f32[128]{0:T(128)S(1)} %get-tuple-element.153) | copy-start | bytes 1540
  83.9 44.2 %copy-start.33 = (f32[128]{0:T(128)}, f32[128]{0:T(128)S(1)}, u32[]{:S(2)}) copy-start(f32[128]{0:T(128)S(1)} %get-tuple-element.154) | copy-start | bytes 1540
  84.0 44.2 %copy-start.36 = (f32[128]{0:T(128)}, f32[128]{0:T(128)S(1)}, u32[]{:S(2)}) copy-start(f32[128]{0:T(128)S(1)} %get-tuple-element.155) | copy-start | bytes 1540
  84.0 44.2 %copy-start.40 = (f32[128]{0:T(128)}, f32[128]{0:T(128)S(1)}, u32[]{:S(2)}) copy-start(f32[128]{0:T(128)S(1)} %get-tuple-element.156) | copy-start | bytes 1540
  85.5 12.4 %copy-start.18 = (bf16[1,16,16,128]{3,2,1,0:T(8,128)(2,1)}, bf16[1,16,16,128]{3,2,1,0:T(8,128)(2,1)S(1)}, u32[]{:S(2)}) copy-start(bf16[1,16,16,128]{3,2,1,0:T(8,128)(2,1)S(1)} %copy.72) | copy-start | bytes 196612
  92.6 32.8 %copy-start.10 = (bf16[256,3,128]{0,2,1:T(8,128)(2,1)}, bf16[256,3,128]{0,2,1:T(8,128)(2,1)S(1)}, u32[]{:S(2)}) copy-start(bf16[256,3,128]{0,2,1:T(8,128)(2,1)S(1)} %copy.63) | copy-start | bytes 589828
  125.7 11.3 %copy-start.20 = (f32[2048]{0:T(1024)}, f32[2048]{0:T(1024)S(1)}, u32[]{:S(2)}) copy-start(f32[2048]{0:T(1024)S(1)} %get-tuple-element.159) | copy-start | bytes 24580
  138.9 8.9 %copy-start.5 = (bf16[2048,128]{0,1:T(8,128)(2,1)S(1)}, bf16[2048,128]{0,1:T(8,128)(2,1)}, u32[]{:S(2)}) copy-start(bf16[2048,128]{0,1:T(8,128)(2,1)} %get-tuple-element.151) | copy-start | bytes 1572868
  138.9 11.3 %copy-start.27 = (f32[4,512]{1,0:T(4,128)S(1)}, f32[4,512]{1,0:T(4,128)}, u32[]{:S(2)}) copy-start(f32[4,512]{1,0:T(4,128)} %get-tuple-element.164) | copy-start | bytes 24580
  138.9 11.3 %copy-start.28 = (f32[4,512]{1,0:T(4,128)S(1)}, f32[4,512]{1,0:T(4,128)}, u32[]{:S(2)}) copy-start(f32[4,512]{1,0:T(4,128)} %get-tuple-element.165) | copy-start | bytes 24580
  138.9 11.3 %copy-start.34 = (f32[128]{0:T(128)S(1)}, f32[128]{0:T(128)}, u32[]{:S(2)}) copy-start(f32[128]{0:T(128)} %copy-done.33) | copy-start | bytes 1540
  138.9 11.3 %copy-start.37 = (f32[128]{0:T(128)S(1)}, f32[128]{0:T(128)}, u32[]{:S(2)}) copy-start(f32[128]{0:T(128)} %copy-done.36) | copy-start | bytes 1540
  138.9 11.3 %copy-start.42 = (pred[4,512]{1,0:T(4,128)(4,1)S(1)}, pred[4,512]{1,0:T(4,128)(4,1)}, u32[]{:S(2)}) copy-start(pred[4,512]{1,0:T(4,128)(4,1)} %convert_compare_fusion) | copy-start | bytes 6148
  138.9 11.3 %copy-start.46 = (pred[128]{0:T(512)(128)(4,1)S(1)}, pred[128]{0:T(512)(128)(4,1)}, u32[]{:S(2)}) copy-start(pred[128]{0:T(512)(128)(4,1)} %copy-done.45) | copy-start | bytes 388
  138.9 11.3 %copy-start.49 = (f32[128]{0:T(128)S(1)}, f32[128]{0:T(128)}, u32[]{:S(2)}) copy-start(f32[128]{0:T(128)} %copy-done.48) | copy-start | bytes 1540
  138.9 11.3 %copy-start.52 = (pred[128]{0:T(512)(128)(4,1)S(1)}, pred[128]{0:T(512)(128)(4,1)}, u32[]{:S(2)}) copy-start(pred[128]{0:T(512)(128)(4,1)} %copy-done.51) | copy-start | bytes 388
  139.0 11.3 %copy-start.55 = (pred[128]{0:T(512)(128)(4,1)S(1)}, pred[128]{0:T(512)(128)(4,1)}, u32[]{:S(2)}) copy-start(pred[128]{0:T(512)(128)(4,1)} %copy-done.54) | copy-start | bytes 388
  158.1 41.7 %copy-start.12 = (f32[2048,1,127]{0,2,1:T(8,128)S(1)}, f32[2048,1,127]{0,2,1:T(8,128)}, u32[]{:S(2)}) copy-start(f32[2048,1,127]{0,2,1:T(8,128)} %get-tuple-element.143) | copy-start | bytes 3121156
  158.9 2.1 copy-start
  161.2 5.0 %copy-start.1 = (f32[512,2048]{1,0:T(8,128)S(1)}, f32[512,2048]{1,0:T(8,128)}, u32[]{:S(2)}) copy-start(f32[512,2048]{1,0:T(8,128)} %copy-done) | copy-start | bytes 12582916 | tf_op jit(solution)/shard_map/while
  166.3 2.1 copy-start.4
  171.5 5.1 %copy-start.1 = (f32[512,2048]{1,0:T(8,128)S(1)}, f32[512,2048]{1,0:T(8,128)}, u32[]{:S(2)}) copy-start(f32[512,2048]{1,0:T(8,128)} %copy-done) | copy-start | bytes 12582916 | tf_op jit(solution)/shard_map/while
  176.6 2.1 copy-start.4
  181.8 5.0 %copy-start.1 = (f32[512,2048]{1,0:T(8,128)S(1)}, f32[512,2048]{1,0:T(8,128)}, u32[]{:S(2)}) copy-start(f32[512,2048]{1,0:T(8,128)} %copy-done) | copy-start | bytes 12582916 | tf_op jit(solution)/shard_map/while
  186.9 2.2 copy-start.4
  189.9 2.1 copy-start
  192.1 5.0 %copy-start.1 = (f32[512,2048]{1,0:T(8,128)S(1)}, f32[512,2048]{1,0:T(8,128)}, u32[]{:S(2)}) copy-start(f32[512,2048]{1,0:T(8,128)} %copy-done) | copy-start | bytes 12582916 | tf_op jit(solution)/shard_map/while
  197.1 2.2 copy-start.4
  199.7 10.6 %copy-start.13 = (f32[2048,1,127]{0,2,1:T(8,128)S(1)}, f32[2048,1,127]{0,2,1:T(8,128)}, u32[]{:S(2)}) copy-start(f32[2048,1,127]{0,2,1:T(8,128)} %get-tuple-element.131) | copy-start | bytes 3121156
  199.8 10.6 %copy-start.14 = (f32[2048,1,127]{0,2,1:T(8,128)S(1)}, f32[2048,1,127]{0,2,1:T(8,128)}, u32[]{:S(2)}) copy-start(f32[2048,1,127]{0,2,1:T(8,128)} %get-tuple-element.133) | copy-start | bytes 3121156
  199.8 10.6 %copy-start.21 = (f32[2048]{0:T(1024)S(1)}, f32[2048]{0:T(1024)}, u32[]{:S(2)}) copy-start(f32[2048]{0:T(1024)} %copy-done.20) | copy-start | bytes 24580
  199.8 10.6 %copy-start.24 = (f32[2048]{0:T(1024)S(1)}, f32[2048]{0:T(1024)}, u32[]{:S(2)}) copy-start(f32[2048]{0:T(1024)} %copy-done.23) | copy-start | bytes 24580
  199.8 10.6 %copy-start.26 = (f32[2048]{0:T(1024)S(1)}, f32[2048]{0:T(1024)}, u32[]{:S(2)}) copy-start(f32[2048]{0:T(1024)} %copy-done.25) | copy-start | bytes 24580
  199.8 10.6 %copy-start.35 = (f32[128]{0:T(128)S(1)}, f32[128]{0:T(128)}, u32[]{:S(2)}) copy-start(f32[128]{0:T(128)} %copy-done.33) | copy-start | bytes 1540
  199.8 10.6 %copy-start.38 = (f32[128]{0:T(128)S(1)}, f32[128]{0:T(128)}, u32[]{:S(2)}) copy-start(f32[128]{0:T(128)} %copy-done.36) | copy-start | bytes 1540
  199.8 10.6 %copy-start.43 = (f32[2048,1,1]{0,2,1:T(1,128)S(1)}, f32[2048,1,1]{0,2,1:T(1,128)}, u32[]{:S(2)}) copy-start(f32[2048,1,1]{0,2,1:T(1,128)} %get-tuple-element.127) | copy-start | bytes 24580
  199.8 10.6 %copy-start.44 = (f32[2048,1,1]{0,2,1:T(1,128)S(1)}, f32[2048,1,1]{0,2,1:T(1,128)}, u32[]{:S(2)}) copy-start(f32[2048,1,1]{0,2,1:T(1,128)} %get-tuple-element.128) | copy-start | bytes 24580
  199.8 10.6 %copy-start.47 = (pred[128]{0:T(512)(128)(4,1)S(1)}, pred[128]{0:T(512)(128)(4,1)}, u32[]{:S(2)}) copy-start(pred[128]{0:T(512)(128)(4,1)} %copy-done.45) | copy-start | bytes 388
  199.8 10.6 %copy-start.50 = (f32[128]{0:T(128)S(1)}, f32[128]{0:T(128)}, u32[]{:S(2)}) copy-start(f32[128]{0:T(128)} %copy-done.48) | copy-start | bytes 1540
  199.9 10.6 %copy-start.53 = (pred[128]{0:T(512)(128)(4,1)S(1)}, pred[128]{0:T(512)(128)(4,1)}, u32[]{:S(2)}) copy-start(pred[128]{0:T(512)(128)(4,1)} %copy-done.51) | copy-start | bytes 388
  199.9 10.6 %copy-start.56 = (pred[128]{0:T(512)(128)(4,1)S(1)}, pred[128]{0:T(512)(128)(4,1)}, u32[]{:S(2)}) copy-start(pred[128]{0:T(512)(128)(4,1)} %copy-done.54) | copy-start | bytes 388
  199.9 10.6 %copy-start.58 = (bf16[4,512,2048]{2,1,0:T(8,128)(2,1)S(1)}, bf16[4,512,2048]{2,1,0:T(8,128)(2,1)}, u32[]{:S(2)}) copy-start(bf16[4,512,2048]{2,1,0:T(8,128)(2,1)} %get-tuple-element.49) | copy-start | bytes 25165828
  219.5 9.9 %slice-start = ((s8[8388608]{0:T(1024)(128)(4,1)}), s8[4194304]{0:T(1024)(128)(4,1)S(1)}, s32[]{:S(2)}) async-start(s8[8388608]{0:T(1024)(128)(4,1)} %bitcast.229), calls=%async_computation.6 | async-start | bytes 8388608
  220.2 9.2 %copy-start.8 = (bf16[1,16,112,128]{3,2,1,0:T(8,128)(2,1)S(1)}, bf16[1,16,112,128]{3,2,1,0:T(8,128)(2,1)}, u32[]{:S(2)}) copy-start(bf16[1,16,112,128]{3,2,1,0:T(8,128)(2,1)} %copy-done.7) | copy-start | bytes 1376260
  220.2 9.2 %copy-start.19 = (bf16[1,16,16,128]{3,2,1,0:T(8,128)(2,1)S(1)}, bf16[1,16,16,128]{3,2,1,0:T(8,128)(2,1)}, u32[]{:S(2)}) copy-start(bf16[1,16,16,128]{3,2,1,0:T(8,128)(2,1)} %copy-done.18) | copy-start | bytes 196612
  220.2 9.2 %slice-start.1 = ((s8[8388608]{0:T(1024)(128)(4,1)}), s8[4194304]{0:T(1024)(128)(4,1)S(1)}, s32[]{:S(2)}) async-start(s8[8388608]{0:T(1024)(128)(4,1)} %bitcast.229), calls=%async_computation.7 | async-start | bytes 8388608
  229.5 2.2 copy-start.16
  229.5 3.0 copy-start.22
  229.5 3.0 copy-start.39
  235.7 20.7 %all-to-all-start.5 = ((bf16[1,256,4,128]{3,2,0,1:T(4,128)(2,1)}), bf16[1,256,4,128]{3,2,0,1:T(4,128)(2,1)S(1)}, u32[]{:S(2)}, u32[]{:S(2)}) async-start(bf16[1,256,4,128]{3,2,0,1:T(4,128)(2,1)} %copy.84), calls=%async_computation.5 | async-start | bytes 524288 | tf_op jit(solution)/shard_map/all_to_all | solution.py:153
  256.4 139.6 %all-to-all-start.4 = ((bf16[1,1792,4,128]{3,2,0,1:T(4,128)(2,1)}), bf16[1,1792,4,128]{3,2,0,1:T(4,128)(2,1)S(1)}, u32[]{:S(2)}, u32[]{:S(2)}) async-start(bf16[1,1792,4,128]{3,2,0,1:T(4,128)(2,1)} %copy.81), calls=%async_computation.4 | async-start | bytes 3670016 | tf_op jit(solution)/shard_map/all_to_all | solution.py:152
  (21 other events, 25.5 us)
where the time goes:
time: 406 us; the launch traced here: 399 us
  blocking collectives  131 us (32%)
  local copies, waits for them, and re-layouts  67.2 us (17%)
  other arithmetic  62.7 us (15%)
  matrix products  51.8 us (13%)
  starting transfers between devices  47.3 us (12%)
  waiting for transfers between devices  35.8 us (9%)
    unnamed x1, blocking collectives  92.2 us
    psum x1, blocking collectives, per_device(): summed = lax.psum(partial_grad, 'seq')  39 us
    unnamed x125, local copies, waits for them, and re-layouts  27.8 us
    unnamed x3, other arithmetic  23.1 us
    all_to_all x1, waiting for transfers between devices, per_device(): lax.all_to_all(img_qkv, 'seq', split_axis=3, concat_axis=1, tiled=True)  21.8 us
    dot_general x4, matrix products, block_step(): lax.dot_general(d_block, value, contract_last, preferred_element_type=jnp...  20.2 us
    all_to_all x1, starting transfers between devices, per_device(): lax.all_to_all(txt_back, 'seq', split_axis=1, concat_axis=3, tiled=True)  12.1 us
    dot_general x1, matrix products, head_pass(): dq_rot = jnp.dot(d_score_all, k_rot, preferred_element_type=jnp.float32)  10.5 us
  transfers between devices with their start and end apart: 6, of which 4 were waited for; matrix products, arithmetic and copies ran while one was open for 12% of the time, Pallas kernels for 0%

commit v1 on v0

v1 whole, which is shorter than its diff:
```python
import functools
import math

import jax
import jax.numpy as jnp
import numpy as np
from jax import lax
from jax.experimental import pallas as pl
from jax.experimental.pallas import tpu as pltpu
from jax.sharding import PartitionSpec as P

HD = 128
GRID_W = 64
EPSILON = 1e-06
F32 = jnp.float32
BF16 = jnp.bfloat16
SCALE = 1.0 / math.sqrt(HD)
LOG2E_SCALE = SCALE * math.log2(math.e)
NT = (((1,), (1,)), ((), ()))
BLK = 128
TXT_B = 16
QB = 256
GRAD_SCALE = 1.0 / math.sqrt(32 * 2048 * 16)
KC = 512


def small_tables(n_rows):
    time_dims = HD // 8
    axis = (HD - time_dims) // 2
    channel = np.arange(HD)
    in_rows = (channel >= time_dims) & (channel < time_dims + axis)
    in_cols = channel >= time_dims + axis
    within = np.where(in_cols, channel - time_dims - axis, channel - time_dims)
    within = np.maximum(within, 0) // 2
    freq = np.power(10000.0, -2.0 * within / axis).astype(np.float32)
    sign = np.where(channel % 2 == 0, -1.0, 1.0)
    rows = np.arange(n_rows, dtype=np.float32)[:, None] * np.where(in_rows, freq, 0)[None, :]
    cols = np.arange(GRID_W, dtype=np.float32)[:, None] * np.where(in_cols, freq, 0)[None, :]
    rows, cols = rows.astype(np.float32).astype(np.float64), cols.astype(np.float32).astype(np.float64)
    out = [np.cos(rows), np.sin(rows) * sign, np.cos(cols), np.sin(cols) * sign]
    return [o.astype(np.float32) for o in out]


def fill_tables(rc, rs, cc, cs, cos_ref, sin_ref):
    lane = lax.broadcasted_iota(jnp.int32, (16, HD), 1)
    is_col = lane >= HD // 8 + (HD - HD // 8) // 2

    def text(b, c):
        cos_ref[b, pl.ds(0, TXT_B), :] = jnp.ones((TXT_B, HD), F32)
        sin_ref[b, pl.ds(0, TXT_B), :] = jnp.zeros((TXT_B, HD), F32)
        return c

    lax.fori_loop(0, 16, text, 0)

    def image(m, c):
        b, off = m // 7, pl.multiple_of(16 + 16 * (m % 7), 16)
        r, col = m // 4, pl.multiple_of(16 * (m % 4), 16)
        cos_ref[b, pl.ds(off, 16), :] = jnp.where(is_col, cc[pl.ds(col, 16), :], rc[pl.ds(r, 1), :])
        sin_ref[b, pl.ds(off, 16), :] = jnp.where(is_col, cs[pl.ds(col, 16), :], rs[pl.ds(r, 1), :])
        return c

    lax.fori_loop(0, 112, image, 0)


def swap_pairs(x):
    lane = lax.broadcasted_iota(jnp.int32, x.shape, x.ndim - 1)
    return jnp.where(lane % 2 == 0, pltpu.roll(x, HD - 1, axis=1), pltpu.roll(x, 1, axis=1))


def normed(x):
    inv = lax.rsqrt(jnp.mean(x * x, axis=-1, keepdims=True) + EPSILON)
    return x * inv, inv


def gain_rows(gains, which):
    row = lax.broadcasted_iota(jnp.int32, (BLK, HD), 0)
    img = jnp.broadcast_to(gains[which : which + 1, :], (BLK, HD))
    txt = jnp.broadcast_to(gains[which + 2 : which + 3, :], (BLK, HD))
    return jnp.where(row < TXT_B, txt, img)


def rope_block(raw, gain, cos, sin):
    hat, _ = normed(raw.astype(F32))
    x = hat * gain
    return (x * cos + swap_pairs(x) * sin).astype(BF16)


def back_block(raw, d_rot, gain, cos, sin):
    hat, inv = normed(raw.astype(F32))
    d_norm = d_rot * cos + swap_pairs(d_rot * sin)
    terms = d_norm * hat
    scaled = d_norm * gain
    middle = jnp.mean(scaled * hat, axis=-1, keepdims=True)
    return ((scaled - hat * middle) * inv).astype(BF16), terms[:TXT_B], terms[TXT_B:]


def fold8(x):
    total = x[0:8]
    for i in range(8, x.shape[0], 8):
        total = total + x[i : i + 8]
    return total


def prep_k(b, kin, vin, gains, cos_ref, sin_ref, kr, krt, vt):
    k = rope_block(kin[b], gain_rows(gains, 1), cos_ref[b], sin_ref[b])
    kr[b] = k
    krt[b] = k.T
    vt[b] = vin[b].T


def prep_q(b, qin, gains, cos_ref, sin_ref, qr):
    qr[b] = rope_block(qin[b], gain_rows(gains, 0), cos_ref[b], sin_ref[b])


def cat_t(ref, c, n):
    return jnp.concatenate([ref[c * n + i] for i in range(n)], axis=1)


def forward(i, kr, vt, qr, eb, oout, inv_l):
    n = KC // BLK
    two = pl.ds(2 * i, 2)
    q = qr[two].reshape(QB, HD)
    total = jnp.zeros((8, QB), F32)
    acc = jnp.zeros((HD, QB), F32)
    for c in range(16 // n):
        keys = kr[c * n : (c + 1) * n].reshape(KC, HD)
        s = lax.dot_general(keys, q, NT, preferred_element_type=F32)
        e = jnp.exp2(s * LOG2E_SCALE)
        total = total + fold8(e)
        e16 = e.astype(BF16)
        eb[i, pl.ds(c * KC, KC), :] = e16
        acc = acc + jnp.dot(cat_t(vt, c, n), e16, preferred_element_type=F32)
    inv = 1.0 / jnp.sum(total, axis=0, keepdims=True)
    inv_l[i] = jnp.broadcast_to(inv, (8, QB))
    oout[two] = (acc * inv).T.astype(BF16).reshape(2, BLK, HD)


def backward(i, first, gin, vin, kr, krt, qr, oout, eb, inv_l, dkacc, dvacc, dqrot):
    n = KC // BLK
    two = pl.ds(2 * i, 2)
    g = gin[two].reshape(QB, HD).astype(F32)
    o = oout[two].reshape(QB, HD).astype(F32)
    inv = inv_l[i][0:1, :]
    delta = jnp.sum((g * o).T, axis=0, keepdims=True) * inv
    gt = (g.T * inv).astype(BF16)
    gs = gt.T
    q = qr[two].reshape(QB, HD)
    acc = jnp.zeros((HD, QB), F32)
    for c in range(16 // n):
        rows = pl.ds(c * KC, KC)
        e16 = eb[i, rows, :]
        values = vin[c * n : (c + 1) * n].reshape(KC, HD)
        dp = jnp.dot(values, gt, preferred_element_type=F32)
        ds = (e16.astype(F32) * (dp - delta)).astype(BF16)
        dv = jnp.dot(e16, gs, preferred_element_type=F32)
        dk = jnp.dot(ds, q, preferred_element_type=F32)
        if first:
            dvacc[rows, :] = dv
            dkacc[rows, :] = dk
        else:
            dvacc[rows, :] += dv
            dkacc[rows, :] += dk
        acc = acc + jnp.dot(cat_t(krt, c, n), ds, preferred_element_type=F32)
    dqrot[...] = (acc * SCALE).T.reshape(2, BLK, HD)


def finish(b, raw, d_rot, which, gains, cos_ref, sin_ref, out, gsum):
    d, txt, img = back_block(raw[b], d_rot, gain_rows(gains, which), cos_ref[b], sin_ref[b])
    out[b] = d
    gsum[which] += fold8(img)
    gsum[which + 2] += fold8(txt)


def attention_kernel(qin, kin, vin, gin, gains, rc, rs, cc, cs, oout, dq, dk, dv, gout,
                     cos_ref, sin_ref, kr, krt, vt, qr, eb, inv_l, dkacc, dvacc, dqrot, gsum):
    fill_tables(rc, rs, cc, cs, cos_ref, sin_ref)
    gsum[...] = jnp.zeros_like(gsum)
    g = gains[...]

    def prep(b, c):
        prep_k(b, kin, vin, g, cos_ref, sin_ref, kr, krt, vt)
        prep_q(b, qin, g, cos_ref, sin_ref, qr)
        return c

    lax.fori_loop(0, 16, prep, 0)
    dkacc[...] = jnp.zeros_like(dkacc)
    dvacc[...] = jnp.zeros_like(dvacc)

    def step(i, c):
        forward(i, kr, vt, qr, eb, oout, inv_l)
        return c

    lax.fori_loop(0, 8, step, 0)

    def step2(i, c):
        backward(i, False, gin, vin, kr, krt, qr, oout, eb, inv_l, dkacc, dvacc, dqrot)
        for j in range(2):
            finish(2 * i + j, qin, dqrot[j], 0, g, cos_ref, sin_ref, dq, gsum)
        return c

    lax.fori_loop(0, 8, step2, 0)

    def last(b, c):
        rows = pl.ds(pl.multiple_of(b * BLK, BLK), BLK)
        finish(b, kin, dkacc[rows, :] * SCALE, 1, g, cos_ref, sin_ref, dk, gsum)
        dv[b] = dvacc[rows, :].astype(BF16)
        return c

    lax.fori_loop(0, 16, last, 0)
    for j in range(4):
        gout[j : j + 1, :] = jnp.sum(gsum[j], axis=0, keepdims=True)


def compute_scratch():
    return [
        pltpu.VMEM((16, BLK, HD), F32), pltpu.VMEM((16, BLK, HD), F32),
        pltpu.VMEM((16, BLK, HD), BF16), pltpu.VMEM((16, HD, BLK), BF16), pltpu.VMEM((16, HD, BLK), BF16),
        pltpu.VMEM((16, BLK, HD), BF16),
        pltpu.VMEM((8, 2048, QB), BF16), pltpu.VMEM((8, 8, QB), F32),
        pltpu.VMEM((2048, HD), F32), pltpu.VMEM((2048, HD), F32),
        pltpu.VMEM((2, BLK, HD), F32), pltpu.VMEM((4, 8, HD), F32),
    ]


def attention(q, k, v, g, gains):
    block = jax.ShapeDtypeStruct((16, BLK, HD), BF16)
    V = pl.BlockSpec(memory_space=pltpu.VMEM)
    return pl.pallas_call(
        attention_kernel,
        out_shape=[block] * 4 + [jax.ShapeDtypeStruct((4, HD), F32)],
        in_specs=[V] * 9, out_specs=[V] * 5,
        scratch_shapes=compute_scratch(),
        compiler_params=pltpu.CompilerParams(vmem_limit_bytes=56 << 20),
    )(q, k, v, g, gains, *[jnp.asarray(t) for t in small_tables(28)])


def spread(n, axis, fn):
    me = lax.axis_index(axis)

    def one(r, c):
        fn(lax.rem(me + r, n))
        return c

    lax.fori_loop(1, n, one, 0)


def barrier(axes):
    sem = pltpu.get_barrier_semaphore()
    for axis, n in axes:
        spread(n, axis, lambda d, axis=axis: pl.semaphore_signal(
            sem, inc=1, device_id={axis: d}, device_id_type=pl.DeviceIdType.MESH))
    pl.semaphore_wait(sem, sum(n - 1 for _, n in axes))


def remote(src, dst, send, recv, axis, d):
    return pltpu.make_async_remote_copy(src, dst, send, recv, device_id={axis: d}, device_id_type=pl.DeviceIdType.MESH)


def wait_bytes(ref, sem):
    pltpu.make_async_copy(ref, ref, sem).wait()


def head_columns(d):
    return pl.ds(pl.multiple_of(d * HD, HD), HD)


def gather_kernel(img, txt, img_cot, txt_cot, qin, kin, vin, gin, send, recv, local):
    me = lax.axis_index("seq")
    barrier((("seq", 16),))
    text, image = pl.ds(0, TXT_B), pl.ds(TXT_B, BLK - TXT_B)

    def pieces(slot, d):
        col = head_columns(d)
        if slot < 3:
            return txt.at[slot, :, col], img.at[slot, :, col]
        return txt_cot.at[:, col], img_cot.at[:, col]

    slots = ((1, kin), (0, qin), (2, vin), (3, gin))
    for slot, ref in slots:
        def push(d, slot=slot, ref=ref):
            t, i = pieces(slot, d)
            remote(t, ref.at[me, text], send.at[slot], recv.at[slot], "seq", d).start()
            remote(i, ref.at[me, image], send.at[slot], recv.at[slot], "seq", d).start()

        spread(16, "seq", push)
        t, i = pieces(slot, me)
        pltpu.make_async_copy(t, ref.at[me, text], local.at[slot]).start()
        pltpu.make_async_copy(i, ref.at[me, image], local.at[slot]).start()
    for slot, ref in slots:
        wait_bytes(ref.at[0], local.at[slot])
        wait_bytes(ref.at[pl.ds(0, 15)], recv.at[slot])
        wait_bytes(ref.at[pl.ds(0, 15)], send.at[slot])


def scatter_kernel(o, dq, dk, dv, part, img_out, txt_out, img_grad, txt_grad, gain,
                   rows, srow, srows, send, recv, local, gsend, grecv):
    me, dp = lax.axis_index("seq"), lax.axis_index("dp")
    barrier((("seq", 16), ("dp", 32)))
    spread(32, "dp", lambda d: remote(part.at[d // 8], rows.at[dp], gsend.at[0], grecv.at[0], "dp", d).start())
    text, image = pl.ds(0, TXT_B), pl.ds(TXT_B, BLK - TXT_B)
    col = head_columns(me)
    slots = ((0, dq), (1, dk), (2, dv), (3, o))

    def target(slot):
        if slot < 3:
            return txt_grad.at[slot, :, col], img_grad.at[slot, :, col]
        return txt_out.at[:, col], img_out.at[:, col]

    for slot, ref in slots:
        t, i = target(slot)

        def push(d, slot=slot, ref=ref, t=t, i=i):
            remote(ref.at[d, text], t, send.at[slot], recv.at[slot], "seq", d).start()
            remote(ref.at[d, image], i, send.at[slot], recv.at[slot], "seq", d).start()

        spread(16, "seq", push)
        pltpu.make_async_copy(ref.at[me, text], t, local.at[slot]).start()
        pltpu.make_async_copy(ref.at[me, image], i, local.at[slot]).start()
    rows[dp] = part[dp // 8]
    wait_bytes(rows.at[pl.ds(0, 31)], grecv.at[0])
    srow[...] = jnp.sum(rows[...], axis=0)
    spread(16, "seq", lambda d: remote(srow, srows.at[me], gsend.at[1], grecv.at[1], "seq", d).start())
    srows[me] = srow[...]
    wait_bytes(srows.at[pl.ds(0, 15)], grecv.at[1])
    total = jnp.sum(srows[...], axis=0) * GRAD_SCALE
    gain[...] = pltpu.roll(jnp.broadcast_to(total, (8, HD)), lax.rem(HD - lax.rem(dp, 8) * 16, HD), axis=1)
    wait_bytes(rows.at[pl.ds(0, 31)], gsend.at[0])
    wait_bytes(srows.at[pl.ds(0, 15)], gsend.at[1])
    for slot, ref in slots:
        wait_bytes(ref.at[0], local.at[slot])
        wait_bytes(ref.at[pl.ds(0, 15)], send.at[slot])
        wait_bytes(ref.at[pl.ds(0, 15)], recv.at[slot])


def per_device(img_qkv, txt_qkv, img_cot, txt_cot, norm_gains):
    img = jnp.transpose(img_qkv[0], (1, 0, 2))
    txt = jnp.transpose(txt_qkv[0], (1, 0, 2))
    any_, vmem = pl.BlockSpec(memory_space=pl.ANY), pl.BlockSpec(memory_space=pltpu.VMEM)
    block = jax.ShapeDtypeStruct((16, BLK, HD), BF16)
    dma = pltpu.SemaphoreType.DMA
    q, k, v, g = pl.pallas_call(
        gather_kernel, out_shape=[block] * 4, in_specs=[any_] * 4, out_specs=[vmem] * 4,
        scratch_shapes=[dma((4,))] * 3,
        compiler_params=pltpu.CompilerParams(collective_id=0, has_side_effects=True, vmem_limit_bytes=16 << 20),
    )(img, txt, img_cot[0], txt_cot[0])
    o, dq, dk, dv, part = attention(q, k, v, g, norm_gains)
    shape = lambda s: jax.ShapeDtypeStruct(s, BF16)
    n_img, n_txt, width = img.shape[1], txt.shape[1], img.shape[2]
    img_out, txt_out, img_grad, txt_grad, gain = pl.pallas_call(
        scatter_kernel,
        out_shape=[shape((n_img, width)), shape((n_txt, width)), shape((3, n_img, width)), shape((3, n_txt, width)),
                   jax.ShapeDtypeStruct((8, HD), F32)],
        in_specs=[vmem] * 5, out_specs=[any_] * 4 + [vmem],
        scratch_shapes=[pltpu.VMEM((32, 1, HD), F32), pltpu.VMEM((1, HD), F32), pltpu.VMEM((16, 1, HD), F32),
                        dma((4,)), dma((4,)), dma((4,)), dma((2,)), dma((2,))],
        compiler_params=pltpu.CompilerParams(collective_id=1, has_side_effects=True, vmem_limit_bytes=16 << 20),
    )(o, dq, dk, dv, part.reshape(4, 1, HD))
    return (img_out[None], txt_out[None], jnp.transpose(img_grad, (1, 0, 2))[None],
            jnp.transpose(txt_grad, (1, 0, 2))[None], gain[0, :16])


def solution(mesh):
    in_specs = (P("dp", "seq", None, None), P("dp", "seq", None, None), P("dp", "seq", None), P("dp", "seq", None), P())
    out_specs = (P("dp", "seq", None), P("dp", "seq", None), P("dp", "seq", None, None), P("dp", "seq", None, None), P("dp"))
    return jax.shard_map(per_device, mesh=mesh, in_specs=in_specs, out_specs=out_specs, check_vma=False)
```

time: 406 us -> 165 us (0.41)
  the two profiles are of different devices: /device:TPU:2 before, /device:TPU:1 now
where the time goes in v1:
time: 165 us; the launch traced here: 164 us
  Pallas kernels  148 us (90%)
  local copies, waits for them, and re-layouts  15.8 us (10%)
    pallas_call x1, Pallas kernels, per_device(): pl.pallas_call(scatter_kernel, out_shape=[shape((n_img, width)), shape((n...  64.8 us
    pallas_call x1, Pallas kernels, per_device(): pl.pallas_call(gather_kernel, out_shape=[block] * 4, in_specs=[any_] * 4,...  52.3 us
    pallas_call x1, Pallas kernels, attention(): pl.pallas_call(attention_kernel, out_shape=[block] * 4 + [jax.ShapeDtypeS...  30.6 us
    unnamed x30, local copies, waits for them, and re-layouts  15.3 us

profile of v1, /device:TPU:1, one launch (start us, length us, event | category | flops | bytes accessed | tf_op | source)
XLA Modules:
  0.0 164.1 jit_solution(11608600991398840246)
XLA Ops:
  0.6 0.0 copy-start
  0.6 1.3 copy-done
  2.0 0.0 copy-start.9
  2.0 1.0 copy-done.9
  3.0 0.0 copy-start.10
  3.0 0.9 copy-done.10
  3.9 0.0 copy-start.11
  3.9 0.8 copy-done.11
  4.8 52.3 %shard_map.128 = (bf16[16,128,128]{2,1,0:T(8,128)(2,1)S(1)}, bf16[16,128,128]{2,1,0:T(8,128)(2,1)S(1)}, bf16[16,128,128]{2,1,0:T(8,128)(2,1)S(1)}, bf16[16,128,128]{2,1,0:T(8,128)(2,1)S(1)}) custom-call(bf16[3,112,2048]{2,1,0:T(8,128)(2,1)S(1)} %bitcast.20, bf16[3,16,2048]{2,1,0:T(8,128)(2,1)S(1)} %bitcast.23, bf16[112,2048]{1,0:T(8,128)(2,1)S(1)} %bitcast.22, ...), custom_call_target="tpu_custom_call" | custom-call | tf_op jit(solution)/shard_map/pallas_call | solution.py:341
  57.0 0.0 copy-start.5
  57.1 0.8 copy-done.5
  57.8 0.0 copy-start.6
  57.8 0.8 copy-done.6
  58.6 0.0 copy-start.7
  58.6 0.8 copy-done.7
  59.4 0.0 copy-start.8
  59.4 0.8 copy-done.8
  60.3 30.6 %shard_map.129 = (bf16[16,128,128]{2,1,0:T(8,128)(2,1)}, bf16[16,128,128]{2,1,0:T(8,128)(2,1)}, bf16[16,128,128]{2,1,0:T(8,128)(2,1)}, bf16[16,128,128]{2,1,0:T(8,128)(2,1)}, f32[4,128]{1,0:T(4,128)}) custom-call(bf16[16,128,128]{2,1,0:T(8,128)(2,1)} %copy-done.5, bf16[16,128,128]{2,1,0:T(8,128)(2,1)} %copy-done.6, bf16[16,128,128]{2,1,0:T(8,128)(2,1)} %copy-done.7, ...), custom_call_target="tpu_custom_call" | custom-call | tf_op jit(solution)/shard_map/pallas_call | solution.py:228
  90.8 0.0 copy-start.1
  90.8 1.0 copy-done.1
  91.9 0.0 copy-start.2
  91.9 1.0 copy-done.2
  92.9 0.0 copy-start.3
  92.9 1.0 copy-done.3
  93.9 0.0 copy-start.4
  93.9 1.0 copy-done.4
  95.0 0.0 copy-start.12
  95.0 0.7 copy-done.12
  95.7 64.8 %shard_map.130 = (bf16[112,2048]{1,0:T(8,128)(2,1)S(1)}, bf16[16,2048]{1,0:T(8,128)(2,1)S(1)}, bf16[3,112,2048]{2,1,0:T(8,128)(2,1)S(1)}, bf16[3,16,2048]{2,1,0:T(8,128)(2,1)S(1)}, f32[8,128]{1,0:T(8,128)S(1)}) custom-call(bf16[16,128,128]{2,1,0:T(8,128)(2,1)S(1)} %copy-done.1, bf16[16,128,128]{2,1,0:T(8,128)(2,1)S(1)} %copy-done.2, ...), custom_call_target="tpu_custom_call" | custom-call | tf_op jit(solution)/shard_map/pallas_call | solution.py:349
  160.4 0.5 slice_bitcast_fusion
  161.0 0.8 copy.18
  161.7 0.6 copy.19
  162.4 1.1 copy.20
  163.4 0.7 copy.21
Async XLA Ops:
  0.6 1.3 copy-start
  2.0 1.0 copy-start.9
  3.0 0.9 copy-start.10
  3.9 0.8 copy-start.11
  57.0 0.8 copy-start.5
  57.8 0.8 copy-start.6
  58.6 0.8 copy-start.7
  59.4 0.8 copy-start.8
  90.8 1.0 copy-start.1
  91.9 1.0 copy-start.2
  92.9 1.0 copy-start.3
  93.9 1.0 copy-start.4
  95.0 0.7 copy-start.12

commit v2 on v1

v2 whole, which is shorter than its diff:
```python
import functools
import math

import jax
import jax.numpy as jnp
import numpy as np
from jax import lax
from jax.experimental import pallas as pl
from jax.experimental.pallas import tpu as pltpu
from jax.sharding import PartitionSpec as P

HD = 128
GRID_W = 64
EPSILON = 1e-06
F32 = jnp.float32
BF16 = jnp.bfloat16
SCALE = 1.0 / math.sqrt(HD)
LOG2E_SCALE = SCALE * math.log2(math.e)
NT = (((1,), (1,)), ((), ()))
BLK = 128
TXT_B = 16
QB = 256
GRAD_SCALE = 1.0 / math.sqrt(32 * 2048 * 16)
KC = 512


def small_tables(n_rows):
    time_dims = HD // 8
    axis = (HD - time_dims) // 2
    channel = np.arange(HD)
    in_rows = (channel >= time_dims) & (channel < time_dims + axis)
    in_cols = channel >= time_dims + axis
    within = np.where(in_cols, channel - time_dims - axis, channel - time_dims)
    within = np.maximum(within, 0) // 2
    freq = np.power(10000.0, -2.0 * within / axis).astype(np.float32)
    sign = np.where(channel % 2 == 0, -1.0, 1.0)
    rows = np.arange(n_rows, dtype=np.float32)[:, None] * np.where(in_rows, freq, 0)[None, :]
    cols = np.arange(GRID_W, dtype=np.float32)[:, None] * np.where(in_cols, freq, 0)[None, :]
    rows, cols = rows.astype(np.float32).astype(np.float64), cols.astype(np.float32).astype(np.float64)
    out = [np.cos(rows), np.sin(rows) * sign, np.cos(cols), np.sin(cols) * sign]
    return [o.astype(np.float32) for o in out]


def fill_tables(rc, rs, cc, cs, cos_ref, sin_ref):
    lane = lax.broadcasted_iota(jnp.int32, (16, HD), 1)
    is_col = lane >= HD // 8 + (HD - HD // 8) // 2

    def text(b, c):
        cos_ref[b, pl.ds(0, TXT_B), :] = jnp.ones((TXT_B, HD), F32)
        sin_ref[b, pl.ds(0, TXT_B), :] = jnp.zeros((TXT_B, HD), F32)
        return c

    lax.fori_loop(0, 16, text, 0)

    def image(m, c):
        b, off = m // 7, pl.multiple_of(16 + 16 * (m % 7), 16)
        r, col = m // 4, pl.multiple_of(16 * (m % 4), 16)
        cos_ref[b, pl.ds(off, 16), :] = jnp.where(is_col, cc[pl.ds(col, 16), :], rc[pl.ds(r, 1), :])
        sin_ref[b, pl.ds(off, 16), :] = jnp.where(is_col, cs[pl.ds(col, 16), :], rs[pl.ds(r, 1), :])
        return c

    lax.fori_loop(0, 112, image, 0)


def swap_pairs(x):
    lane = lax.broadcasted_iota(jnp.int32, x.shape, x.ndim - 1)
    return jnp.where(lane % 2 == 0, pltpu.roll(x, HD - 1, axis=1), pltpu.roll(x, 1, axis=1))


def normed(x):
    inv = lax.rsqrt(jnp.mean(x * x, axis=-1, keepdims=True) + EPSILON)
    return x * inv, inv


def gain_rows(gains, which):
    row = lax.broadcasted_iota(jnp.int32, (BLK, HD), 0)
    img = jnp.broadcast_to(gains[which : which + 1, :], (BLK, HD))
    txt = jnp.broadcast_to(gains[which + 2 : which + 3, :], (BLK, HD))
    return jnp.where(row < TXT_B, txt, img)


def rope_block(raw, gain, cos, sin):
    hat, _ = normed(raw.astype(F32))
    x = hat * gain
    return (x * cos + swap_pairs(x) * sin).astype(BF16)


def back_block(raw, d_rot, gain, cos, sin):
    hat, inv = normed(raw.astype(F32))
    d_norm = d_rot * cos + swap_pairs(d_rot * sin)
    terms = d_norm * hat
    scaled = d_norm * gain
    middle = jnp.mean(scaled * hat, axis=-1, keepdims=True)
    return ((scaled - hat * middle) * inv).astype(BF16), terms[:TXT_B], terms[TXT_B:]


def fold8(x):
    total = x[0:8]
    for i in range(8, x.shape[0], 8):
        total = total + x[i : i + 8]
    return total


def cat_t(ref, c, n):
    return jnp.concatenate([ref[c * n + i] for i in range(n)], axis=1)


def forward(i, kr, vt, qr, eb, oout, inv_l):
    n = KC // BLK
    two = pl.ds(2 * i, 2)
    q = qr[two].reshape(QB, HD)
    total = jnp.zeros((8, QB), F32)
    acc = jnp.zeros((HD, QB), F32)
    for c in range(16 // n):
        keys = kr[c * n : (c + 1) * n].reshape(KC, HD)
        s = lax.dot_general(keys, q, NT, preferred_element_type=F32)
        e = jnp.exp2(s * LOG2E_SCALE)
        total = total + fold8(e)
        e16 = e.astype(BF16)
        eb[i, pl.ds(c * KC, KC), :] = e16
        acc = acc + jnp.dot(cat_t(vt, c, n), e16, preferred_element_type=F32)
    inv = 1.0 / jnp.sum(total, axis=0, keepdims=True)
    inv_l[i] = jnp.broadcast_to(inv, (8, QB))
    oout[two] = (acc * inv).T.astype(BF16).reshape(2, BLK, HD)


def backward(i, first, gin, vin, kr, krt, qr, oout, eb, inv_l, dkacc, dvacc, dqrot):
    n = KC // BLK
    two = pl.ds(2 * i, 2)
    g = gin[two].reshape(QB, HD).astype(F32)
    o = oout[two].reshape(QB, HD).astype(F32)
    inv = inv_l[i][0:1, :]
    delta = jnp.sum((g * o).T, axis=0, keepdims=True) * inv
    gt = (g.T * inv).astype(BF16)
    gs = gt.T
    q = qr[two].reshape(QB, HD)
    acc = jnp.zeros((HD, QB), F32)
    for c in range(16 // n):
        rows = pl.ds(c * KC, KC)
        e16 = eb[i, rows, :]
        values = vin[c * n : (c + 1) * n].reshape(KC, HD)
        dp = jnp.dot(values, gt, preferred_element_type=F32)
        ds = (e16.astype(F32) * (dp - delta)).astype(BF16)
        dv = jnp.dot(e16, gs, preferred_element_type=F32)
        dk = jnp.dot(ds, q, preferred_element_type=F32)
        if first:
            dvacc[rows, :] = dv
            dkacc[rows, :] = dk
        else:
            dvacc[rows, :] += dv
            dkacc[rows, :] += dk
        acc = acc + jnp.dot(cat_t(krt, c, n), ds, preferred_element_type=F32)
    dqrot[...] = (acc * SCALE).T.reshape(2, BLK, HD)


def finish(b, raw, d_rot, which, gains, cos_ref, sin_ref, out, gsum):
    d, txt, img = back_block(raw[b], d_rot, gain_rows(gains, which), cos_ref[...], sin_ref[...])
    out[b] = d
    gsum[which] += fold8(img)
    gsum[which + 2] += fold8(txt)


def spread(n, axis, fn):
    me = lax.axis_index(axis)

    def one(r, c):
        fn(lax.rem(me + r, n))
        return c

    lax.fori_loop(1, n, one, 0)


def barrier(axes):
    sem = pltpu.get_barrier_semaphore()
    for axis, n in axes:
        spread(n, axis, lambda d, axis=axis: pl.semaphore_signal(
            sem, inc=1, device_id={axis: d}, device_id_type=pl.DeviceIdType.MESH))
    pl.semaphore_wait(sem, sum(n - 1 for _, n in axes))


def remote(src, dst, send, recv, axis, d):
    return pltpu.make_async_remote_copy(src, dst, send, recv, device_id={axis: d}, device_id_type=pl.DeviceIdType.MESH)


def wait_bytes(ref, sem):
    pltpu.make_async_copy(ref, ref, sem).wait()


def head_columns(d):
    return pl.ds(pl.multiple_of(d * HD, HD), HD)


def joint_kernel(img, txt, img_cot, txt_cot, gains, rc, rs, cc, cs,
                 img_out, txt_out, img_grad, txt_grad, gain,
                 qin, kin, vin, gin, oout, dq, dk, dv,
                 cos_ref, sin_ref, kr, krt, vt, qr, eb, inv_l, dkacc, dvacc, dqrot, gsum,
                 part, rows, srow, srows, send, recv, osend, orecv, olocal, gsend, grecv):
    me, dp = lax.axis_index("seq"), lax.axis_index("dp")
    barrier((("seq", 16), ("dp", 32)))
    text, image = pl.ds(0, TXT_B), pl.ds(TXT_B, BLK - TXT_B)

    def pieces(slot, d):
        col = head_columns(d)
        if slot < 3:
            return txt.at[slot, :, col], img.at[slot, :, col]
        return txt_cot.at[:, col], img_cot.at[:, col]

    for slot, ref in ((1, kin), (2, vin), (0, qin), (3, gin)):
        def push(r, c, slot=slot, ref=ref):
            d = lax.rem(me + r, 16)
            t, i = pieces(slot, d)
            remote(t, ref.at[r, text], send.at[slot], recv.at[slot, r], "seq", d).start()
            remote(i, ref.at[r, image], send.at[slot], recv.at[slot, r], "seq", d).start()
            return c

        t, i = pieces(slot, me)
        pltpu.make_async_copy(t, ref.at[0, text], recv.at[slot, 0]).start()
        pltpu.make_async_copy(i, ref.at[0, image], recv.at[slot, 0]).start()
        lax.fori_loop(1, 16, push, 0)

    def source(r):
        return lax.rem(me + 16 - r, 16)

    col = head_columns(me)

    def targets(slot):
        if slot < 3:
            return txt_grad.at[slot, :, col], img_grad.at[slot, :, col]
        return txt_out.at[:, col], img_out.at[:, col]

    def push_back(slot, ref, r):
        t, i = targets(slot)

        @pl.when(r == 0)
        def _():
            pltpu.make_async_copy(ref.at[0, text], t, olocal.at[slot]).start()
            pltpu.make_async_copy(ref.at[0, image], i, olocal.at[slot]).start()

        @pl.when(r > 0)
        def _():
            d = source(r)
            remote(ref.at[r, text], t, osend.at[slot], orecv.at[slot], "seq", d).start()
            remote(ref.at[r, image], i, osend.at[slot], orecv.at[slot], "seq", d).start()

    fill_tables(rc, rs, cc, cs, cos_ref, sin_ref)
    gsum[...] = jnp.zeros_like(gsum)
    dkacc[...] = jnp.zeros_like(dkacc)
    dvacc[...] = jnp.zeros_like(dvacc)
    g = gains[...]

    def take_k(r, c):
        wait_bytes(kin.at[r], recv.at[1, r])
        s = source(r)
        k = rope_block(kin[r], gain_rows(g, 1), cos_ref[s], sin_ref[s])
        kr[r] = k
        krt[r] = k.T
        return c

    lax.fori_loop(0, 16, take_k, 0)

    def take_v(r, c):
        wait_bytes(vin.at[r], recv.at[2, r])
        vt[r] = vin[r].T
        return c

    lax.fori_loop(0, 16, take_v, 0)

    def ahead(i, c):
        for j in range(2):
            r = 2 * i + j
            wait_bytes(qin.at[r], recv.at[0, r])
            s = source(r)
            qr[r] = rope_block(qin[r], gain_rows(g, 0), cos_ref[s], sin_ref[s])
        forward(i, kr, vt, qr, eb, oout, inv_l)

        @pl.when(i > 0)
        def _():
            push_back(3, oout, 2 * i - 2)
            push_back(3, oout, 2 * i - 1)

        return c

    lax.fori_loop(0, 8, ahead, 0)

    def back(i, c):
        for j in range(2):
            wait_bytes(gin.at[2 * i + j], recv.at[3, 2 * i + j])

        @pl.when(i == 0)
        def _():
            push_back(3, oout, 14)
            push_back(3, oout, 15)

        backward(i, False, gin, vin, kr, krt, qr, oout, eb, inv_l, dkacc, dvacc, dqrot)
        for j in range(2):
            r = 2 * i + j
            s = source(r)
            finish(r, qin, dqrot[j], 0, g, cos_ref.at[s], sin_ref.at[s], dq, gsum)

        @pl.when(i > 0)
        def _():
            push_back(0, dq, 2 * i - 2)
            push_back(0, dq, 2 * i - 1)

        return c

    lax.fori_loop(0, 8, back, 0)

    def last_v(r, c):
        dv[r] = dvacc[pl.ds(pl.multiple_of(r * BLK, BLK), BLK), :].astype(BF16)
        return c

    lax.fori_loop(0, 16, last_v, 0)
    push_back(0, dq, 14)
    push_back(0, dq, 15)

    def last_k(r, c):
        s = source(r)
        push_back(2, dv, r)
        finish(r, kin, dkacc[pl.ds(pl.multiple_of(r * BLK, BLK), BLK), :] * SCALE, 1, g, cos_ref.at[s], sin_ref.at[s], dk, gsum)
        return c

    lax.fori_loop(0, 16, last_k, 0)
    for j in range(4):
        part[j] = jnp.sum(gsum[j], axis=0, keepdims=True)

    def send_k(r, c):
        push_back(1, dk, r)
        return c

    rows[dp] = part[dp // 8]
    lax.fori_loop(0, 8, send_k, 0)
    spread(32, "dp", lambda d: remote(part.at[d // 8], rows.at[dp], gsend.at[0], grecv.at[0], "dp", d).start())
    lax.fori_loop(8, 16, send_k, 0)
    wait_bytes(rows.at[pl.ds(0, 31)], grecv.at[0])
    srow[...] = jnp.sum(rows[...], axis=0)
    srows[me] = srow[...]
    for slot, ref in ((0, qin), (1, kin), (2, vin), (3, gin)):
        wait_bytes(ref.at[pl.ds(0, 15)], send.at[slot])
    spread(16, "seq", lambda d: remote(srow, srows.at[me], gsend.at[1], grecv.at[1], "seq", d).start())
    wait_bytes(srows.at[pl.ds(0, 15)], grecv.at[1])
    total = jnp.sum(srows[...], axis=0) * GRAD_SCALE
    gain[...] = pltpu.roll(jnp.broadcast_to(total, (8, HD)), lax.rem(HD - lax.rem(dp, 8) * 16, HD), axis=1)
    wait_bytes(rows.at[pl.ds(0, 31)], gsend.at[0])
    wait_bytes(srows.at[pl.ds(0, 15)], gsend.at[1])
    for slot, ref in ((0, dq), (1, dk), (2, dv), (3, oout)):
        wait_bytes(ref.at[0], olocal.at[slot])
        wait_bytes(ref.at[pl.ds(0, 15)], osend.at[slot])
        wait_bytes(ref.at[pl.ds(0, 15)], orecv.at[slot])


def compute_scratch():
    return [
        pltpu.VMEM((16, BLK, HD), F32), pltpu.VMEM((16, BLK, HD), F32),
        pltpu.VMEM((16, BLK, HD), BF16), pltpu.VMEM((16, HD, BLK), BF16), pltpu.VMEM((16, HD, BLK), BF16),
        pltpu.VMEM((16, BLK, HD), BF16),
        pltpu.VMEM((8, 2048, QB), BF16), pltpu.VMEM((8, 8, QB), F32),
        pltpu.VMEM((2048, HD), F32), pltpu.VMEM((2048, HD), F32),
        pltpu.VMEM((2, BLK, HD), F32), pltpu.VMEM((4, 8, HD), F32),
    ]


def per_device(img_qkv, txt_qkv, img_cot, txt_cot, norm_gains):
    img = jnp.transpose(img_qkv[0], (1, 0, 2))
    txt = jnp.transpose(txt_qkv[0], (1, 0, 2))
    any_, vmem = pl.BlockSpec(memory_space=pl.ANY), pl.BlockSpec(memory_space=pltpu.VMEM)
    dma = pltpu.SemaphoreType.DMA
    shape = lambda s: jax.ShapeDtypeStruct(s, BF16)
    n_img, n_txt, width = img.shape[1], txt.shape[1], img.shape[2]
    img_out, txt_out, img_grad, txt_grad, gain = pl.pallas_call(
        joint_kernel,
        out_shape=[shape((n_img, width)), shape((n_txt, width)), shape((3, n_img, width)), shape((3, n_txt, width)),
                   jax.ShapeDtypeStruct((8, HD), F32)],
        in_specs=[any_] * 4 + [vmem] * 5, out_specs=[any_] * 4 + [vmem],
        scratch_shapes=[pltpu.VMEM((16, BLK, HD), BF16)] * 8 + compute_scratch() + [
            pltpu.VMEM((4, 1, HD), F32), pltpu.VMEM((32, 1, HD), F32), pltpu.VMEM((1, HD), F32), pltpu.VMEM((16, 1, HD), F32),
            dma((4,)), dma((4, 16)), dma((4,)), dma((4,)), dma((4,)), dma((2,)), dma((2,))],
        compiler_params=pltpu.CompilerParams(collective_id=0, has_side_effects=True, vmem_limit_bytes=56 << 20),
    )(img, txt, img_cot[0], txt_cot[0], norm_gains, *[jnp.asarray(t) for t in small_tables(28)])
    return (img_out[None], txt_out[None], jnp.transpose(img_grad, (1, 0, 2))[None],
            jnp.transpose(txt_grad, (1, 0, 2))[None], gain[0, :16])


def solution(mesh):
    in_specs = (P("dp", "seq", None, None), P("dp", "seq", None, None), P("dp", "seq", None), P("dp", "seq", None), P())
    out_specs = (P("dp", "seq", None), P("dp", "seq", None), P("dp", "seq", None, None), P("dp", "seq", None, None), P("dp"))
    return jax.shard_map(per_device, mesh=mesh, in_specs=in_specs, out_specs=out_specs, check_vma=False)
```

time: 165 us -> 123 us (0.75)
  Pallas kernels: 148 us -> 114 us
  local copies, waits for them, and re-layouts: 15.8 us -> 7.77 us
    pallas_call x3 -> x1, Pallas kernels: 148 us -> 114 us  [per_device(): pl.pallas_call(joint_kernel, out_shape=[shape((n_img, width)), shape((n_t...]
    unnamed x30 -> x6, local copies, waits for them, and re-layouts: 15.3 us -> 6.58 us
where the time goes in v2:
time: 123 us
  Pallas kernels  114 us (93%)
  local copies, waits for them, and re-layouts  7.77 us (6%)
    pallas_call x1, Pallas kernels, per_device(): pl.pallas_call(joint_kernel, out_shape=[shape((n_img, width)), shape((n_t...  114 us
    unnamed x6, local copies, waits for them, and re-layouts  6.58 us

profile of v2, /device:TPU:1, one launch (start us, length us, event | category | flops | bytes accessed | tf_op | source)
XLA Modules:
  0.0 122.6 jit_solution(7623737955615355883)
XLA Ops:
  0.6 114.2 %shard_map.128 = (bf16[112,2048]{1,0:T(8,128)(2,1)}, bf16[16,2048]{1,0:T(8,128)(2,1)}, bf16[3,112,2048]{2,1,0:T(8,128)(2,1)}, bf16[3,16,2048]{2,1,0:T(8,128)(2,1)}, f32[8,128]{1,0:T(8,128)}) custom-call(bf16[3,112,2048]{2,1,0:T(8,128)(2,1)} %bitcast.18, bf16[3,16,2048]{2,1,0:T(8,128)(2,1)} %bitcast.22, bf16[112,2048]{1,0:T(8,128)(2,1)} %bitcast.20, ...), custom_call_target="tpu_custom_call" | custom-call | tf_op jit(solution)/shard_map/pallas_call | solution.py:370
  114.8 1.2 slice_bitcast_fusion
  116.0 1.8 %copy.18 = bf16[1,112,2048]{2,1,0:T(8,128)(2,1)} copy(bf16[1,112,2048]{2,1,0:T(8,128)(2,1)} %bitcast.21) | data formatting | bytes 917504
  117.9 1.5 %copy.19 = bf16[1,16,2048]{2,1,0:T(8,128)(2,1)} copy(bf16[1,16,2048]{2,1,0:T(8,128)(2,1)} %bitcast.25) | data formatting | bytes 131072
  119.3 0.0 copy-start
  119.3 2.6 %copy.20 = bf16[1,112,3,2048]{3,1,2,0:T(8,128)(2,1)} copy(bf16[1,112,3,2048]{3,1,2,0:T(8,128)(2,1)} %bitcast.19) | data formatting | bytes 2752512
  121.9 0.0 copy-done
  121.9 0.7 copy.21
Async XLA Ops:
  119.3 2.6 %copy-start = (bf16[3,16,2048]{2,1,0:T(8,128)(2,1)S(1)}, bf16[3,16,2048]{2,1,0:T(8,128)(2,1)}, u32[]{:S(2)}) copy-start(bf16[3,16,2048]{2,1,0:T(8,128)(2,1)} %get-tuple-element.13) | copy-start | bytes 589828

commit v3 on v2

--- a/solution.py
+++ b/solution.py
@@ -18,6 +18,7 @@
 LOG2E_SCALE = SCALE * math.log2(math.e)
 NT = (((1,), (1,)), ((), ()))
 BLK = 128
+DP_STAGES = ((2, 4, 6), (1, 16, 17), (8,))
 TXT_B = 16
 QB = 256
 GRAD_SCALE = 1.0 / math.sqrt(32 * 2048 * 16)
@@ -160,6 +161,13 @@
     gsum[which + 2] += fold8(txt)
 
 
+def flip(i, bits):
+    for b in (1, 2, 4, 8, 16):
+        if bits & b:
+            i = i + b - 2 * b * (i // b % 2)
+    return i
+
+
 def spread(n, axis, fn):
     me = lax.axis_index(axis)
 
@@ -170,12 +178,18 @@
     lax.fori_loop(1, n, one, 0)
 
 
-def barrier(axes):
+def barrier():
     sem = pltpu.get_barrier_semaphore()
-    for axis, n in axes:
-        spread(n, axis, lambda d, axis=axis: pl.semaphore_signal(
-            sem, inc=1, device_id={axis: d}, device_id_type=pl.DeviceIdType.MESH))
-    pl.semaphore_wait(sem, sum(n - 1 for _, n in axes))
+
+    def greet(axis, d):
+        pl.semaphore_signal(sem, inc=1, device_id={axis: d}, device_id_type=pl.DeviceIdType.MESH)
+
+    spread(16, "seq", lambda d: greet("seq", d))
+    dp = lax.axis_index("dp")
+    for stage in DP_STAGES:
+        for bits in stage:
+            greet("dp", flip(dp, bits))
+    pl.semaphore_wait(sem, 15 + sum(len(stage) for stage in DP_STAGES))
 
 
 def remote(src, dst, send, recv, axis, d):
@@ -190,13 +204,12 @@
     return pl.ds(pl.multiple_of(d * HD, HD), HD)
 
 
-def joint_kernel(img, txt, img_cot, txt_cot, gains, rc, rs, cc, cs,
-                 img_out, txt_out, img_grad, txt_grad, gain,
+def joint_kernel(img, txt, img_cot, txt_cot, gains, rc, rs, cc, cs, back_out, gain,
                  qin, kin, vin, gin, oout, dq, dk, dv,
                  cos_ref, sin_ref, kr, krt, vt, qr, eb, inv_l, dkacc, dvacc, dqrot, gsum,
                  part, rows, srow, srows, send, recv, osend, orecv, olocal, gsend, grecv):
     me, dp = lax.axis_index("seq"), lax.axis_index("dp")
-    barrier((("seq", 16), ("dp", 32)))
+    barrier()
     text, image = pl.ds(0, TXT_B), pl.ds(TXT_B, BLK - TXT_B)
 
     def pieces(slot, d):
@@ -223,24 +236,16 @@
 
     col = head_columns(me)
 
-    def targets(slot):
-        if slot < 3:
-            return txt_grad.at[slot, :, col], img_grad.at[slot, :, col]
-        return txt_out.at[:, col], img_out.at[:, col]
-
     def push_back(slot, ref, r):
-        t, i = targets(slot)
+        there = back_out.at[slot, :, col]
 
         @pl.when(r == 0)
         def _():
-            pltpu.make_async_copy(ref.at[0, text], t, olocal.at[slot]).start()
-            pltpu.make_async_copy(ref.at[0, image], i, olocal.at[slot]).start()
+            pltpu.make_async_copy(ref.at[0], there, olocal.at[slot]).start()
 
         @pl.when(r > 0)
         def _():
-            d = source(r)
-            remote(ref.at[r, text], t, osend.at[slot], orecv.at[slot], "seq", d).start()
-            remote(ref.at[r, image], i, osend.at[slot], orecv.at[slot], "seq", d).start()
+            remote(ref.at[r], there, osend.at[slot], orecv.at[slot], "seq", source(r)).start()
 
     fill_tables(rc, rs, cc, cs, cos_ref, sin_ref)
     gsum[...] = jnp.zeros_like(gsum)
@@ -306,47 +311,72 @@
 
     lax.fori_loop(0, 8, back, 0)
 
-    def last_v(r, c):
-        dv[r] = dvacc[pl.ds(pl.multiple_of(r * BLK, BLK), BLK), :].astype(BF16)
-        return c
-
-    lax.fori_loop(0, 16, last_v, 0)
     push_back(0, dq, 14)
     push_back(0, dq, 15)
 
-    def last_k(r, c):
+    def last(r, c):
         s = source(r)
-        push_back(2, dv, r)
-        finish(r, kin, dkacc[pl.ds(pl.multiple_of(r * BLK, BLK), BLK), :] * SCALE, 1, g, cos_ref.at[s], sin_ref.at[s], dk, gsum)
-        return c
-
-    lax.fori_loop(0, 16, last_k, 0)
+        rows_r = pl.ds(pl.multiple_of(r * BLK, BLK), BLK)
+        dv[r] = dvacc[rows_r, :].astype(BF16)
+        finish(r, kin, dkacc[rows_r, :] * SCALE, 1, g, cos_ref.at[s], sin_ref.at[s], dk, gsum)
+        return c
+
+    lax.fori_loop(0, 16, last, 0)
     for j in range(4):
-        part[j] = jnp.sum(gsum[j], axis=0, keepdims=True)
-
-    def send_k(r, c):
-        push_back(1, dk, r)
-        return c
-
-    rows[dp] = part[dp // 8]
-    lax.fori_loop(0, 8, send_k, 0)
-    spread(32, "dp", lambda d: remote(part.at[d // 8], rows.at[dp], gsend.at[0], grecv.at[0], "dp", d).start())
-    lax.fori_loop(8, 16, send_k, 0)
-    wait_bytes(rows.at[pl.ds(0, 31)], grecv.at[0])
-    srow[...] = jnp.sum(rows[...], axis=0)
+        part[0, j : j + 1] = jnp.sum(gsum[j], axis=0, keepdims=True)
+
+    def push_some(slot, ref, a, b):
+        def one(r, c):
+            push_back(slot, ref, r)
+            return c
+
+        lax.fori_loop(a, b, one, 0)
+
+    bulk = ((2, dv, 0, 8), (2, dv, 8, 16), (1, dk, 0, 8), (1, dk, 8, 16))
+    for n, stage in enumerate(DP_STAGES):
+        for m, bits in enumerate(stage):
+            remote(part.at[n], rows.at[n, m], gsend.at[n], grecv.at[n], "dp", flip(dp, bits)).start()
+        push_some(*bulk[n])
+        here = rows.at[n, pl.ds(0, len(stage))]
+        wait_bytes(here, grecv.at[n])
+        total = part[n]
+        for m in range(len(stage)):
+            total = total + rows[n, m]
+        part[n + 1] = total
+    srow[...] = part[3]
+    spread(16, "seq", lambda d: remote(srow, srows.at[me], gsend.at[3], grecv.at[3], "seq", d).start())
+    push_some(*bulk[3])
     srows[me] = srow[...]
+    wait_bytes(srows.at[pl.ds(0, 15)], grecv.at[3])
+    total = jnp.sum(srows[...], axis=0) * GRAD_SCALE
+    line = jnp.zeros((1, HD), F32)
+    for j in range(4):
+        line = jnp.where(dp // 8 == j, total[j : j + 1], line)
+    gain[...] = pltpu.roll(jnp.broadcast_to(line, (8, HD)), lax.rem(HD - lax.rem(dp, 8) * 16, HD), axis=1)
+    for n, stage in enumerate(DP_STAGES):
+        wait_bytes(rows.at[n, pl.ds(0, len(stage))], gsend.at[n])
+    wait_bytes(srows.at[pl.ds(0, 15)], gsend.at[3])
     for slot, ref in ((0, qin), (1, kin), (2, vin), (3, gin)):
         wait_bytes(ref.at[pl.ds(0, 15)], send.at[slot])
-    spread(16, "seq", lambda d: remote(srow, srows.at[me], gsend.at[1], grecv.at[1], "seq", d).start())
-    wait_bytes(srows.at[pl.ds(0, 15)], grecv.at[1])
-    total = jnp.sum(srows[...], axis=0) * GRAD_SCALE
-    gain[...] = pltpu.roll(jnp.broadcast_to(total, (8, HD)), lax.rem(HD - lax.rem(dp, 8) * 16, HD), axis=1)
-    wait_bytes(rows.at[pl.ds(0, 31)], gsend.at[0])
-    wait_bytes(srows.at[pl.ds(0, 15)], gsend.at[1])
-    for slot, ref in ((0, dq), (1, dk), (2, dv), (3, oout)):
+    for slot, ref in ((3, oout), (0, dq), (2, dv), (1, dk)):
         wait_bytes(ref.at[0], olocal.at[slot])
         wait_bytes(ref.at[pl.ds(0, 15)], osend.at[slot])
         wait_bytes(ref.at[pl.ds(0, 15)], orecv.at[slot])
+
+
+def emit_kernel(back_out, gain, img_out, txt_out, img_grad, txt_grad, gain_out, sems):
+    text, image, grads = pl.ds(0, TXT_B), pl.ds(TXT_B, BLK - TXT_B), pl.ds(0, 3)
+    copies = [
+        pltpu.make_async_copy(back_out.at[grads, image], img_grad, sems.at[0]),
+        pltpu.make_async_copy(back_out.at[3, image], img_out, sems.at[1]),
+        pltpu.make_async_copy(back_out.at[grads, text], txt_grad, sems.at[2]),
+        pltpu.make_async_copy(back_out.at[3, text], txt_out, sems.at[3]),
+    ]
+    for copy in copies:
+        copy.start()
+    gain_out[...] = gain[0:1, 0:16]
+    for copy in copies:
+        copy.wait()
 
 
 def compute_scratch():
@@ -367,18 +397,24 @@
     dma = pltpu.SemaphoreType.DMA
     shape = lambda s: jax.ShapeDtypeStruct(s, BF16)
     n_img, n_txt, width = img.shape[1], txt.shape[1], img.shape[2]
-    img_out, txt_out, img_grad, txt_grad, gain = pl.pallas_call(
+    back_out, gain = pl.pallas_call(
         joint_kernel,
+        out_shape=[pltpu.VMEM((4, BLK, width), BF16), pltpu.VMEM((8, HD), F32)],
+        in_specs=[any_] * 4 + [vmem] * 5, out_specs=[vmem] * 2,
+        scratch_shapes=[pltpu.VMEM((16, BLK, HD), BF16)] * 8 + compute_scratch() + [
+            pltpu.VMEM((4, 4, HD), F32), pltpu.VMEM((3, 3, 4, HD), F32), pltpu.VMEM((4, HD), F32), pltpu.VMEM((16, 4, HD), F32),
+            dma((4,)), dma((4, 16)), dma((4,)), dma((4,)), dma((4,)), dma((4,)), dma((4,))],
+        compiler_params=pltpu.CompilerParams(collective_id=0, has_side_effects=True, vmem_limit_bytes=58 << 20),
+    )(img, txt, img_cot[0], txt_cot[0], norm_gains, *[jnp.asarray(t) for t in small_tables(28)])
+    img_out, txt_out, img_grad, txt_grad, gain_out = pl.pallas_call(
+        emit_kernel,
         out_shape=[shape((n_img, width)), shape((n_txt, width)), shape((3, n_img, width)), shape((3, n_txt, width)),
-                   jax.ShapeDtypeStruct((8, HD), F32)],
-        in_specs=[any_] * 4 + [vmem] * 5, out_specs=[any_] * 4 + [vmem],
-        scratch_shapes=[pltpu.VMEM((16, BLK, HD), BF16)] * 8 + compute_scratch() + [
-            pltpu.VMEM((4, 1, HD), F32), pltpu.VMEM((32, 1, HD), F32), pltpu.VMEM((1, HD), F32), pltpu.VMEM((16, 1, HD), F32),
-            dma((4,)), dma((4, 16)), dma((4,)), dma((4,)), dma((4,)), dma((2,)), dma((2,))],
-        compiler_params=pltpu.CompilerParams(collective_id=0, has_side_effects=True, vmem_limit_bytes=56 << 20),
-    )(img, txt, img_cot[0], txt_cot[0], norm_gains, *[jnp.asarray(t) for t in small_tables(28)])
+                   jax.ShapeDtypeStruct((1, 16), F32)],
+        in_specs=[vmem] * 2, out_specs=[any_] * 4 + [vmem], scratch_shapes=[dma((4,))],
+        compiler_params=pltpu.CompilerParams(vmem_limit_bytes=8 << 20),
+    )(back_out, gain)
     return (img_out[None], txt_out[None], jnp.transpose(img_grad, (1, 0, 2))[None],
-            jnp.transpose(txt_grad, (1, 0, 2))[None], gain[0, :16])
+            jnp.transpose(txt_grad, (1, 0, 2))[None], gain_out.reshape(16))
 
 
 def solution(mesh):

time: 123 us -> 111 us (0.902)
  local copies, waits for them, and re-layouts: 7.77 us -> 0 us
  Pallas kernels: 114 us -> 110 us
    unnamed x6 -> x0, local copies, waits for them, and re-layouts: 6.58 us -> none
    pallas_call x1 -> x2, Pallas kernels: 114 us -> 110 us  [the longest x1 109 us: per_device(): pl.pallas_call(joint_kernel, out_shape=[pltpu.VMEM((4, BLK, width), BF16)...]
where the time goes in v3:
time: 111 us
  Pallas kernels  110 us (99%)
    pallas_call x1, Pallas kernels, per_device(): pl.pallas_call(joint_kernel, out_shape=[pltpu.VMEM((4, BLK, width), BF16)...  109 us

profile of v3, /device:TPU:1, one launch (start us, length us, event | category | flops | bytes accessed | tf_op | source)
XLA Modules:
  0.0 111.1 jit_solution(1770386815367032658)
XLA Ops:
  0.6 108.6 %shard_map.128 = (bf16[4,128,2048]{2,1,0:T(8,128)(2,1)S(1)}, f32[8,128]{1,0:T(8,128)S(1)}) custom-call(bf16[3,112,2048]{2,1,0:T(8,128)(2,1)} %bitcast.17, bf16[3,16,2048]{2,1,0:T(8,128)(2,1)} %bitcast.19, bf16[112,2048]{1,0:T(8,128)(2,1)} %bitcast.18, bf16[16,2048]{1,0:T(8,128)(2,1)} %bitcast.20, f32[4,128]{1,0:T(4,128)} %gains.1, ...), custom_call_target="tpu_custom_call" | custom-call | tf_op jit(solution)/shard_map/pallas_call | solution.py:400
  109.3 1.8 %shard_map.129 = (bf16[112,2048]{1,0:T(8,128)(2,1)}, bf16[16,2048]{1,0:T(8,128)(2,1)}, bf16[3,112,2048]{2,1,0:T(8,128)(2,1)}, bf16[3,16,2048]{2,1,0:T(8,128)(2,1)}, f32[1,16]{1,0:T(1,128)}) custom-call(bf16[4,128,2048]{2,1,0:T(8,128)(2,1)S(1)} %get-tuple-element.12.back_out, f32[8,128]{1,0:T(8,128)S(1)} %get-tuple-element.13.gain), custom_call_target="tpu_custom_call" | custom-call | tf_op jit(solution)/shard_map/pallas_call | solution.py:409

commit v4 on v3

--- a/solution.py
+++ b/solution.py
@@ -327,7 +327,7 @@
 
     def push_some(slot, ref, a, b):
         def one(r, c):
-            push_back(slot, ref, r)
+            push_back(slot, ref, lax.rem(16 - r, 16))
             return c
 
         lax.fori_loop(a, b, one, 0)

time: 111 us -> 108 us (0.973); the launches traced: 111 us -> 107 us
  Pallas kernels: 110 us -> 106 us
    pallas_call x1, Pallas kernels: 109 us -> 104 us  [per_device(): pl.pallas_call(joint_kernel, out_shape=[pltpu.VMEM((4, BLK, width), BF16)...]
where the time goes in v4:
time: 108 us; the launch traced here: 107 us
  Pallas kernels  106 us (98%)
    pallas_call x1, Pallas kernels, per_device(): pl.pallas_call(joint_kernel, out_shape=[pltpu.VMEM((4, BLK, width), BF16)...  104 us

profile of v4, /device:TPU:1, one launch (start us, length us, event | category | flops | bytes accessed | tf_op | source)
XLA Modules:
  0.0 106.9 jit_solution(16738778480945644436)
XLA Ops:
  0.6 104.4 %shard_map.128 = (bf16[4,128,2048]{2,1,0:T(8,128)(2,1)S(1)}, f32[8,128]{1,0:T(8,128)S(1)}) custom-call(bf16[3,112,2048]{2,1,0:T(8,128)(2,1)} %bitcast.17, bf16[3,16,2048]{2,1,0:T(8,128)(2,1)} %bitcast.19, bf16[112,2048]{1,0:T(8,128)(2,1)} %bitcast.18, bf16[16,2048]{1,0:T(8,128)(2,1)} %bitcast.20, f32[4,128]{1,0:T(4,128)} %gains.1, ...), custom_call_target="tpu_custom_call" | custom-call | tf_op jit(solution)/shard_map/pallas_call | solution.py:400
  105.0 1.8 %shard_map.129 = (bf16[112,2048]{1,0:T(8,128)(2,1)}, bf16[16,2048]{1,0:T(8,128)(2,1)}, bf16[3,112,2048]{2,1,0:T(8,128)(2,1)}, bf16[3,16,2048]{2,1,0:T(8,128)(2,1)}, f32[1,16]{1,0:T(1,128)}) custom-call(bf16[4,128,2048]{2,1,0:T(8,128)(2,1)S(1)} %get-tuple-element.12.back_out, f32[8,128]{1,0:T(8,128)S(1)} %get-tuple-element.13.gain), custom_call_target="tpu_custom_call" | custom-call | tf_op jit(solution)/shard_map/pallas_call | solution.py:409
